TPU v7x, 32 devices: a whole 2x2x4 slice. The times are simulated.
32 devices in a mesh: dp: 8 (over y, x, core), tensor: 4 (over z).
Axes of the slice: x: 2, y: 2, z: 4, core: 2. Of those that a mesh axis runs over, the one named last changes fastest.
Arguments:
- inputs: bfloat16 [8192, 1024], P(('dp', 'tensor')), may hold values from -6 to 6
- segments: int32 [8, 1024], P('dp'), may hold values from 0 to 3, never falling along the last dimension, each value on 1 to 512 neighbouring positions
- query_weight: bfloat16 [1024, 1024], P(None, 'tensor'), may hold values from -0.1875 to 0.1875
- key_weight: bfloat16 [1024, 1024], P(None, 'tensor'), may hold values from -0.1875 to 0.1875
- value_weight: bfloat16 [1024, 1024], P(None, 'tensor'), may hold values from -0.1875 to 0.1875
- gate_weight: bfloat16 [1024, 1024], P(None, 'tensor'), may hold values from -0.1875 to 0.1875
- out_weight: bfloat16 [1024, 1024], P('tensor'), may hold values from -0.1875 to 0.1875
- left_weight: bfloat16 [1024, 2816], P(None, 'tensor'), may hold values from -0.1875 to 0.1875
- right_weight: bfloat16 [1024, 2816], P(None, 'tensor'), may hold values from -0.1875 to 0.1875
- down_weight: bfloat16 [2816, 1024], P('tensor'), may hold values from -0.109375 to 0.109375
- norm_first: float32 [1024], replicated, may hold values from 0.1 to 1.9
- norm_second: float32 [1024], replicated, may hold values from 0.1 to 1.9
- cotangent: bfloat16 [8192, 1024], P(('dp', 'tensor')), may hold values from -6 to 6
Outputs:
- block_out: bfloat16 [8192, 1024], P(('dp', 'tensor'))
- block_grad: bfloat16 [8192, 1024], P(('dp', 'tensor'))
- query_grad: float32 [1024, 1024], P(None, 'tensor')
- key_grad: float32 [1024, 1024], P(None, 'tensor')
- value_grad: float32 [1024, 1024], P(None, 'tensor')
- gate_grad: float32 [1024, 1024], P(None, 'tensor')
- out_grad: float32 [1024, 1024], P('tensor')
- left_grad: float32 [1024, 2816], P(None, 'tensor')
- right_grad: float32 [1024, 2816], P(None, 'tensor')
- down_grad: float32 [2816, 1024], P('tensor')
- first_grad: float32 [1024], replicated
- second_grad: float32 [1024], replicated
Inputs may be any that keep to these rules, and one draw needn't show every extreme that they name: `segments`: each row holds 4 documents; numbers never fall along a row; each document has 1 to 512 tokens and one of each row exactly 512.
All inputs are finite; a program needn't handle non-finite values.
Results may differ from a plain program's by a relative error of at most 0.02.
Values may be sent and summed in bfloat16 or wider, within the bound.
A program may use at most 128 MiB of HBM per device.

v0:
```python
import jax
import jax.numpy as jnp
from jax import lax
from jax.sharding import PartitionSpec as P

D = 1024
HEADS = 16


EPS = 1e-05


def rms_scale(values):
    return lax.rsqrt(jnp.mean(values * values, axis=-1, keepdims=True) + EPS)


def norm_back(grad_normed, values, scale, gain):
    weighted = grad_normed * gain
    return scale * weighted - values * scale * scale * scale * jnp.mean(
        weighted * values, axis=-1, keepdims=True
    )


def attention_scores(query_pos, key_pos, doc_mask):
    raw_scores = jnp.einsum(
        "rthd,rshd->rhts", query_pos, key_pos, preferred_element_type=jnp.float32
    )
    return jnp.where(doc_mask[:, None], raw_scores, 0.0).astype(jnp.bfloat16)


def per_device(
    inputs,
    segments,
    query_weight,
    key_weight,
    value_weight,
    gate_weight,
    out_weight,
    left_weight,
    right_weight,
    down_weight,
    norm_first,
    norm_second,
    cotangent,
):
    own_rows = inputs.astype(jnp.float32)
    rows_here, length = segments.shape
    all_tokens = rows_here * length
    local_width = query_weight.shape[1]
    head_size = D // HEADS
    heads_here = local_width // head_size
    four_shape = (rows_here, length, heads_here, head_size)
    scale_one = rms_scale(own_rows)
    normed_own = (own_rows * scale_one * norm_first).astype(jnp.bfloat16)
    normed_all = lax.all_gather(normed_own, "tensor", axis=0, tiled=True)
    joined_weight = jnp.concatenate((query_weight, key_weight, value_weight, gate_weight), axis=1)
    projected = jnp.dot(normed_all, joined_weight, preferred_element_type=jnp.float32)
    query_raw = projected[:, :local_width]
    key_raw = projected[:, local_width : 2 * local_width]
    value_raw = projected[:, 2 * local_width : 3 * local_width]
    gate_raw = projected[:, 3 * local_width :]
    query_pos = jax.nn.softplus(query_raw).astype(jnp.bfloat16).reshape(four_shape)
    key_pos = jax.nn.softplus(key_raw).astype(jnp.bfloat16).reshape(four_shape)
    value_pos = value_raw.astype(jnp.bfloat16).reshape(four_shape)
    later = lax.broadcasted_iota(jnp.int32, (length, length), 0) >= lax.broadcasted_iota(
        jnp.int32, (length, length), 1
    )
    doc_mask = (segments[:, :, None] == segments[:, None, :]) & later[None]
    scores = attention_scores(query_pos, key_pos, doc_mask)
    mixed_heads = jnp.einsum(
        "rhts,rshd->rthd", scores, value_pos, preferred_element_type=jnp.float32
    )
    head_scale = rms_scale(mixed_heads)
    head_norm = (mixed_heads * head_scale).reshape(all_tokens, local_width)
    gate_open = jax.nn.sigmoid(gate_raw)
    gated = (head_norm * gate_open).astype(jnp.bfloat16)
    branch = lax.psum_scatter(
        jnp.dot(gated, out_weight, preferred_element_type=jnp.float32),
        "tensor",
        scatter_dimension=0,
        tiled=True,
    )
    residual = own_rows + branch
    scale_two = rms_scale(residual)
    second_own = (residual * scale_two * norm_second).astype(jnp.bfloat16)
    second_all = lax.all_gather(second_own, "tensor", axis=0, tiled=True)
    left_out = jnp.dot(second_all, left_weight, preferred_element_type=jnp.float32)
    right_out = jnp.dot(second_all, right_weight, preferred_element_type=jnp.float32)
    product = (left_out * right_out).astype(jnp.bfloat16)
    ffn_share = lax.psum_scatter(
        jnp.dot(product, down_weight, preferred_element_type=jnp.float32).astype(jnp.bfloat16),
        "tensor",
        scatter_dimension=0,
        tiled=True,
    ).astype(jnp.float32)
    block_out = (residual + ffn_share).astype(jnp.bfloat16)
    upstream = cotangent.astype(jnp.float32)
    down_in = lax.all_gather(cotangent, "tensor", axis=0, tiled=True)
    down_grad = jnp.einsum("tf,td->fd", product, down_in, preferred_element_type=jnp.float32)
    prod_grad = jnp.einsum("td,fd->tf", down_in, down_weight, preferred_element_type=jnp.float32)
    left_back = (prod_grad * right_out).astype(jnp.bfloat16)
    right_back = (prod_grad * left_out).astype(jnp.bfloat16)
    left_grad = jnp.einsum("tc,tf->cf", second_all, left_back, preferred_element_type=jnp.float32)
    right_grad = jnp.einsum("tc,tf->cf", second_all, right_back, preferred_element_type=jnp.float32)
    second_back = lax.psum_scatter(
        jnp.einsum("tf,cf->tc", left_back, left_weight, preferred_element_type=jnp.float32)
        + jnp.einsum("tf,cf->tc", right_back, right_weight, preferred_element_type=jnp.float32),
        "tensor",
        scatter_dimension=0,
        tiled=True,
    )
    second_part = jnp.sum(second_back * residual * scale_two, axis=0)
    resid_grad = upstream + norm_back(second_back, residual, scale_two, norm_second)
    mixer_in = lax.all_gather(resid_grad.astype(jnp.bfloat16), "tensor", axis=0, tiled=True)
    out_grad = jnp.einsum("tc,td->cd", gated, mixer_in, preferred_element_type=jnp.float32)
    gated_back = jnp.einsum("td,cd->tc", mixer_in, out_weight, preferred_element_type=jnp.float32)
    gate_back = (gated_back * head_norm * gate_open * (1.0 - gate_open)).astype(jnp.bfloat16)
    norm_grad = (gated_back * gate_open).reshape(four_shape)
    mixed_back = (
        head_scale * norm_grad
        - mixed_heads
        * head_scale
        * head_scale
        * head_scale
        * jnp.mean(norm_grad * mixed_heads, axis=-1, keepdims=True)
    ).astype(jnp.bfloat16)
    scores_again = attention_scores(query_pos, key_pos, doc_mask)
    value_back = jnp.einsum(
        "rhts,rthd->rshd", scores_again, mixed_back, preferred_element_type=jnp.float32
    ).astype(jnp.bfloat16)
    score_back = jnp.einsum(
        "rthd,rshd->rhts", mixed_back, value_pos, preferred_element_type=jnp.float32
    )
    score_back = jnp.where(doc_mask[:, None], score_back, 0.0).astype(jnp.bfloat16)
    query_back = jnp.einsum(
        "rhts,rshd->rthd", score_back, key_pos, preferred_element_type=jnp.float32
    )
    query_back = (query_back * jax.nn.sigmoid(query_raw.reshape(four_shape))).astype(jnp.bfloat16)
    key_back = jnp.einsum(
        "rhts,rthd->rshd", score_back, query_pos, preferred_element_type=jnp.float32
    )
    key_back = (key_back * jax.nn.sigmoid(key_raw.reshape(four_shape))).astype(jnp.bfloat16)
    back_all = jnp.concatenate(
        (
            query_back.reshape(all_tokens, local_width),
            key_back.reshape(all_tokens, local_width),
            value_back.reshape(all_tokens, local_width),
            gate_back,
        ),
        axis=1,
    )
    joined_grad = jnp.einsum("tc,tq->cq", normed_all, back_all, preferred_element_type=jnp.float32)
    query_grad = joined_grad[:, :local_width]
    key_grad = joined_grad[:, local_width : 2 * local_width]
    value_grad = joined_grad[:, 2 * local_width : 3 * local_width]
    gate_grad = joined_grad[:, 3 * local_width :]
    first_back = lax.psum_scatter(
        jnp.einsum("tq,cq->tc", back_all, joined_weight, preferred_element_type=jnp.float32).astype(
            jnp.bfloat16
        ),
        "tensor",
        scatter_dimension=0,
        tiled=True,
    ).astype(jnp.float32)
    first_part = jnp.sum(first_back * own_rows * scale_one, axis=0)
    block_grad = (resid_grad + norm_back(first_back, own_rows, scale_one, norm_first)).astype(
        jnp.bfloat16
    )
    query_grad, key_grad, value_grad, gate_grad, out_grad, left_grad, right_grad, down_grad = (
        lax.psum(
            (
                query_grad,
                key_grad,
                value_grad,
                gate_grad,
                out_grad,
                left_grad,
                right_grad,
                down_grad,
            ),
            "dp",
        )
    )
    first_grad, second_grad = lax.psum((first_part, second_part), ("dp", "tensor"))
    return (
        block_out,
        block_grad,
        query_grad,
        key_grad,
        value_grad,
        gate_grad,
        out_grad,
        left_grad,
        right_grad,
        down_grad,
        first_grad,
        second_grad,
    )


def solution(mesh):
    return jax.shard_map(
        per_device,
        mesh=mesh,
        in_specs=(
            P(("dp", "tensor"), None),
            P("dp", None),
            P(None, "tensor"),
            P(None, "tensor"),
            P(None, "tensor"),
            P(None, "tensor"),
            P("tensor", None),
            P(None, "tensor"),
            P(None, "tensor"),
            P("tensor", None),
            P(),
            P(),
            P(("dp", "tensor"), None),
        ),
        out_specs=(
            P(("dp", "tensor"), None),
            P(("dp", "tensor"), None),
            P(None, "tensor"),
            P(None, "tensor"),
            P(None, "tensor"),
            P(None, "tensor"),
            P("tensor", None),
            P(None, "tensor"),
            P(None, "tensor"),
            P("tensor", None),
            P(),
            P(),
        ),
        check_vma=False,
    )
```

profile of v0, /device:TPU:0, one launch (start us, length us, event | category | flops | bytes accessed | tf_op | source)
XLA Modules:
  0.0 714.0 jit_solution(3099241303663253236)
XLA Ops:
  14.3 45.8 %all-gather.5.cloned.1.call-done = bf16[1024,1024]{1,0:T(8,128)(2,1)} async-done(((bf16[256,1024]{1,0:T(8,128)(2,1)}), bf16[1024,1024]{1,0:T(8,128)(2,1)}) %all-gather.5.cloned.1.call-update) | async-done | bytes 2097168 | tf_op jit(solution)/shard_map/all_gather | solution.py:55
  60.0 4.7 fusion.34
  68.7 2.7 multiply_reduce_fusion.4
  73.5 2.7 fusion.35
  76.2 75.6 %reduce-scatter.5.cloned.1.call-done = f32[256,1024]{1,0:T(8,128)} async-done(((f32[1024,1024]{1,0:T(8,128)}), f32[256,1024]{1,0:T(8,128)}) %reduce-scatter.5.cloned.1.call-update) | async-done | bytes 1048592 | tf_op jit(solution)/shard_map/reduce_scatter | solution.py:77
  156.5 45.8 %all-gather.7.cloned.1.call-done = bf16[1024,1024]{1,0:T(8,128)(2,1)} async-done(((bf16[256,1024]{1,0:T(8,128)(2,1)}), bf16[1024,1024]{1,0:T(8,128)(2,1)}) %all-gather.7.cloned.1.call-update) | async-done | bytes 2097168 | tf_op jit(solution)/shard_map/all_gather | solution.py:86
  202.3 5.4 fusion.36
  207.7 3.3 fusion.37
  211.0 37.5 %all-gather.9.cloned.1.call-done = bf16[1024,1024]{1,0:T(8,128)(2,1)} async-done(((bf16[256,1024]{1,0:T(8,128)(2,1)}), bf16[1024,1024]{1,0:T(8,128)(2,1)}) %all-gather.9.cloned.1.call-update) | async-done | bytes 2097168 | tf_op jit(solution)/shard_map/all_gather | solution.py:98
  248.5 6.3 multiply_convert_fusion
  257.2 4.0 convolution_add_fusion
  261.3 75.6 %reduce-scatter.9.cloned.1.call-done = f32[256,1024]{1,0:T(8,128)} async-done(((f32[1024,1024]{1,0:T(8,128)}), f32[256,1024]{1,0:T(8,128)}) %reduce-scatter.9.cloned.1.call-update) | async-done | bytes 1048592 | tf_op jit(solution)/shard_map/reduce_scatter | solution.py:105
  341.2 46.4 %all-gather.11.cloned.1.call-done = bf16[1024,1024]{1,0:T(8,128)(2,1)} async-done(((bf16[256,1024]{1,0:T(8,128)(2,1)}), bf16[1024,1024]{1,0:T(8,128)(2,1)}) %all-gather.11.cloned.1.call-update) | async-done | bytes 2097168 | tf_op jit(solution)/shard_map/all_gather | solution.py:114
  387.5 4.1 fusion.32
  392.2 5.1 convolution_convert_fusion.2
  405.1 3.7 convolution_convert_fusion
  409.2 4.6 convolution_convert_fusion.1
  413.8 5.4 fusion.41
  419.3 3.2 fusion.42
  422.5 3.2 fusion.40
  432.6 19.0 %reduce-scatter.11.cloned.1.call-done = bf16[256,1024]{1,0:T(8,128)(2,1)} async-done(((bf16[1024,1024]{1,0:T(8,128)(2,1)}), bf16[256,1024]{1,0:T(8,128)(2,1)}) %reduce-scatter.11.cloned.1.call-update) | async-done | bytes 524304 | tf_op jit(solution)/shard_map/reduce_scatter | solution.py:157
  453.6 42.2 %all-reduce = (f32[1024]{0:T(1024)}, f32[1024]{0:T(1024)}) all-reduce(f32[1024]{0:T(1024)} %get-tuple-element.14, f32[1024]{0:T(1024)S(1)} %copy-done.47), channel_id=1, replica_groups=mesh['dp'=8,'tensor'=4] {'dp','tensor'}, use_global_device_ids=true, to_apply=%region_19.20 | all-reduce | flops 2048 | bytes 16384 | tf_op jit(solution)/shard_map/psum | solution.py:184
  498.2 3.2 fusion.13
  501.4 191.3 %all-reduce.4.cloned.1.call-done = (f32[1024,256]{1,0:T(8,128)}, f32[1024,256]{1,0:T(8,128)}, f32[1024,256]{1,0:T(8,128)}, f32[1024,256]{1,0:T(8,128)}, f32[256,...) async-done(((f32[1024,256]{1,0:T(8,128)}, f32[1024,256]{1,0:T(8,128)}, f32[1024,256]{1,0:T(8,128)}, f32[1024,256]{1,0:T(8,128)}, ...) | async-done | bytes 13893648 | tf_op jit(solution)/shard_map/psum | solution.py:170
  (175 shorter events, 58.3 us)
Async XLA Ops:
  7.2 241.3 %copy-start = (bf16[704,1024]{1,0:T(8,128)(2,1)S(1)}, bf16[704,1024]{1,0:T(8,128)(2,1)}, u32[]{:S(2)}) copy-start(bf16[704,1024]{1,0:T(8,128)(2,1)} %param.22) | copy-start | bytes 4325380
  7.2 52.8 %all-gather.5.cloned.1.call-start = ((), (), s32[]{:S(2)}) async-start(), calls=%async_computation.4 | async-start | bytes 2621440 | tf_op jit(solution)/shard_map/all_gather | solution.py:55
  11.3 140.6 %reduce-scatter.5.cloned.1.call-start = ((), (), s32[]{:S(2)}) async-start(), calls=%async_computation.5 | async-start | bytes 5242880 | tf_op jit(solution)/shard_map/reduce_scatter | solution.py:77
  14.3 51.7 %copy-start.25 = (pred[1024,1024]{1,0:T(8,128)(4,1)}, pred[1024,1024]{1,0:T(8,128)(4,1)S(1)}, u32[]{:S(2)}) copy-start(pred[1024,1024]{1,0:T(8,128)(4,1)S(1)} %fusion) | copy-start | bytes 3145732
  64.7 7.4 %copy-start.14 = (f32[1024,1024]{0,1:T(8,128)}, f32[1024,1024]{0,1:T(8,128)S(1)}, u32[]{:S(2)}) copy-start(f32[1024,1024]{0,1:T(8,128)S(1)} %fusion.34) | copy-start | bytes 12582916
  76.2 126.1 %all-gather.7.cloned.1.call-start = ((), (), s32[]{:S(2)}) async-start(), calls=%async_computation.6 | async-start | bytes 2621440 | tf_op jit(solution)/shard_map/all_gather | solution.py:86
  155.7 92.8 %all-gather.9.cloned.1.call-start = ((), (), s32[]{:S(2)}) async-start(), calls=%async_computation.8 | async-start | bytes 2621440 | tf_op jit(solution)/shard_map/all_gather | solution.py:98
  156.2 180.6 %reduce-scatter.9.cloned.1.call-start = ((), (), s32[]{:S(2)}) async-start(), calls=%async_computation.9 | async-start | bytes 5242880 | tf_op jit(solution)/shard_map/reduce_scatter | solution.py:105
  202.3 5.4 copy-start.51
  202.3 5.4 copy-start.54
  248.5 6.4 copy-start.53
  261.2 126.3 %all-gather.11.cloned.1.call-start = ((), (), s32[]{:S(2)}) async-start(), calls=%async_computation.10 | async-start | bytes 2621440 | tf_op jit(solution)/shard_map/all_gather | solution.py:114
  340.9 110.7 %reduce-scatter.11.cloned.1.call-start = ((), (), s32[]{:S(2)}) async-start(), calls=%async_computation.11 | async-start | bytes 2621440 | tf_op jit(solution)/shard_map/reduce_scatter | solution.py:157
  391.6 12.7 %copy-start.56 = (bf16[1024,256]{0,1:T(8,128)(2,1)}, bf16[1024,256]{0,1:T(8,128)(2,1)S(1)}, u32[]{:S(2)}) copy-start(bf16[1024,256]{0,1:T(8,128)(2,1)S(1)} %get-tuple-element.29) | copy-start | bytes 1572868
  408.9 89.3 %reduce-scatter.7.cloned.1.call-start = ((), (), s32[]{:S(2)}) async-start(), calls=%async_computation.7 | async-start | bytes 2621440 | tf_op jit(solution)/shard_map/reduce_scatter | solution.py:90
  413.8 278.9 %all-reduce.4.cloned.1.call-start = ((), (), s32[]{:S(2)}) async-start(), calls=%async_computation.12 | async-start | bytes 27787264 | tf_op jit(solution)/shard_map/psum | solution.py:170
  413.8 5.5 copy-start.11
  413.8 5.5 copy-start.52
  432.5 19.0 %copy-start.2 = (bf16[256,1024]{1,0:T(8,128)(2,1)S(1)}, bf16[256,1024]{1,0:T(8,128)(2,1)}, u32[]{:S(2)}) copy-start(bf16[256,1024]{1,0:T(8,128)(2,1)} %param.13) | copy-start | bytes 1572868
  432.5 19.0 %copy-start.42 = (f32[1024]{0:T(1024)S(1)}, f32[1024]{0:T(1024)}, u32[]{:S(2)}) copy-start(f32[1024]{0:T(1024)} %param.23) | copy-start | bytes 12292
  432.5 21.0 %copy-start.47 = (f32[1024]{0:T(1024)S(1)}, f32[1024]{0:T(1024)}, u32[]{:S(2)}) copy-start(f32[1024]{0:T(1024)} %get-tuple-element.12) | copy-start | bytes 12292
  432.5 65.6 %copy-start.8 = (bf16[256,1024]{1,0:T(8,128)(2,1)S(1)}, bf16[256,1024]{1,0:T(8,128)(2,1)}, u32[]{:S(2)}) copy-start(bf16[256,1024]{1,0:T(8,128)(2,1)} %param.25) | copy-start | bytes 1572868
  432.6 65.6 %copy-start.41 = (f32[1024]{0:T(1024)S(1)}, f32[1024]{0:T(1024)}, u32[]{:S(2)}) copy-start(f32[1024]{0:T(1024)} %param.24) | copy-start | bytes 12292
  432.6 65.6 %copy-start.45 = (f32[256]{0:T(256)S(1)}, f32[256]{0:T(256)}, u32[]{:S(2)}) copy-start(f32[256]{0:T(256)} %copy-done.43) | copy-start | bytes 3076
  (43 other events, 110.0 us)
Sparse Core Ops, SparseCore 0:
  11.4 48.6 all-gather.4
  76.3 75.4 reduce-scatter.4
  155.8 46.4 all-gather.6
  203.8 44.6 all-gather.8
  261.4 75.4 reduce-scatter.8
  341.0 46.4 all-gather.10
  409.0 42.5 reduce-scatter.10
  454.0 44.1 reduce-scatter.6
  504.2 188.4 all-reduce.3
where the time goes:
time: 722 us; the launch traced here: 714 us
  waiting for transfers between devices  539 us (75%)
  matrix products  74 us (10%)
  blocking collectives  42.2 us (6%)
  local copies, waits for them, and re-layouts  24 us (3%)
  other arithmetic  18.6 us (3%)
  between operations  14.9 us (2%)
    psum x1, waiting for transfers between devices, per_device(): lax.psum((query_grad, key_grad, value_grad, gate_grad, out_grad, left_gra...  191 us
    reduce_scatter x1, waiting for transfers between devices, per_device(): lax.psum_scatter(jnp.dot(gated, out_weight, preferred_element_type=jnp.fl...  75.6 us
    reduce_scatter x1, waiting for transfers between devices, per_device(): lax.psum_scatter(jnp.einsum('tf,cf->tc', left_back, left_weight, preferre...  75.6 us
    all_gather x1, waiting for transfers between devices, per_device(): lax.all_gather(resid_grad.astype(jnp.bfloat16), 'tensor', axis=0, tiled=T...  46.4 us
    all_gather x1, waiting for transfers between devices, per_device(): second_all = lax.all_gather(second_own, 'tensor', axis=0, tiled=True)  45.8 us
    all_gather x1, waiting for transfers between devices, per_device(): normed_all = lax.all_gather(normed_own, 'tensor', axis=0, tiled=True)  45.8 us
    psum x1, blocking collectives, per_device(): lax.psum((first_part, second_part), ('dp', 'tensor'))  42.2 us
    all_gather x1, waiting for transfers between devices, per_device(): down_in = lax.all_gather(cotangent, 'tensor', axis=0, tiled=True)  37.5 us
  transfers between devices with their start and end apart: 9, of which 9 were waited for; matrix products, arithmetic and copies ran while one was open for 5% of the time, Pallas kernels for 0%

commit v1 on v0

--- a/solution.py
+++ b/solution.py
@@ -75,11 +75,11 @@
     gate_open = jax.nn.sigmoid(gate_raw)
     gated = (head_norm * gate_open).astype(jnp.bfloat16)
     branch = lax.psum_scatter(
-        jnp.dot(gated, out_weight, preferred_element_type=jnp.float32),
-        "tensor",
-        scatter_dimension=0,
-        tiled=True,
-    )
+        jnp.dot(gated, out_weight, preferred_element_type=jnp.float32).astype(jnp.bfloat16),
+        "tensor",
+        scatter_dimension=0,
+        tiled=True,
+    ).astype(jnp.float32)
     residual = own_rows + branch
     scale_two = rms_scale(residual)
     second_own = (residual * scale_two * norm_second).astype(jnp.bfloat16)
@@ -103,12 +103,14 @@
     left_grad = jnp.einsum("tc,tf->cf", second_all, left_back, preferred_element_type=jnp.float32)
     right_grad = jnp.einsum("tc,tf->cf", second_all, right_back, preferred_element_type=jnp.float32)
     second_back = lax.psum_scatter(
-        jnp.einsum("tf,cf->tc", left_back, left_weight, preferred_element_type=jnp.float32)
-        + jnp.einsum("tf,cf->tc", right_back, right_weight, preferred_element_type=jnp.float32),
-        "tensor",
-        scatter_dimension=0,
-        tiled=True,
-    )
+        (
+            jnp.einsum("tf,cf->tc", left_back, left_weight, preferred_element_type=jnp.float32)
+            + jnp.einsum("tf,cf->tc", right_back, right_weight, preferred_element_type=jnp.float32)
+        ).astype(jnp.bfloat16),
+        "tensor",
+        scatter_dimension=0,
+        tiled=True,
+    ).astype(jnp.float32)
     second_part = jnp.sum(second_back * residual * scale_two, axis=0)
     resid_grad = upstream + norm_back(second_back, residual, scale_two, norm_second)
     mixer_in = lax.all_gather(resid_grad.astype(jnp.bfloat16), "tensor", axis=0, tiled=True)
@@ -167,16 +169,20 @@
         jnp.bfloat16
     )
     query_grad, key_grad, value_grad, gate_grad, out_grad, left_grad, right_grad, down_grad = (
-        lax.psum(
-            (
-                query_grad,
-                key_grad,
-                value_grad,
-                gate_grad,
-                out_grad,
-                left_grad,
-                right_grad,
-                down_grad,
+        total.astype(jnp.float32)
+        for total in lax.psum(
+            tuple(
+                part.astype(jnp.bfloat16)
+                for part in (
+                    query_grad,
+                    key_grad,
+                    value_grad,
+                    gate_grad,
+                    out_grad,
+                    left_grad,
+                    right_grad,
+                    down_grad,
+                )
             ),
             "dp",
         )

time: 722 us -> 566 us (0.78)
  waiting for transfers between devices: 539 us -> 384 us
  local copies, waits for them, and re-layouts: 24 us -> 9.13 us
  other arithmetic: 18.6 us -> 33 us
    psum x1, waiting for transfers between devices: 191 us -> 101 us  [per_device(): lax.psum(tuple((part.astype(jnp.bfloat16) for part in (query_grad, key_gr...]
    reduce_scatter x1, waiting for transfers between devices: 75.6 us -> 42.7 us  [per_device(): lax.psum_scatter(jnp.dot(gated, out_weight, preferred_element_type=jnp.fl...]
    reduce_scatter x1, waiting for transfers between devices: 75.6 us -> 42.7 us  [per_device(): lax.psum_scatter((jnp.einsum('tf,cf->tc', left_back, left_weight, preferr...]
    unnamed x127 -> x109, local copies, waits for them, and re-layouts: 21.8 us -> 7.62 us
    reduce_scatter x1, waiting for transfers between devices: 19 us -> 33 us  [per_device(): lax.psum_scatter(jnp.einsum('tq,cq->tc', back_all, joined_weight, preferr...]
    convert_element_type x0 -> x8, other arithmetic: none -> 13.3 us  [per_device(): total.astype(jnp.float32)]
    all_gather x1, waiting for transfers between devices: 46.4 us -> 34.6 us  [per_device(): lax.all_gather(resid_grad.astype(jnp.bfloat16), 'tensor', axis=0, tiled=T...]
  transfers between devices with their start and end apart: 9 -> 9, of which waited for: 9 -> 9; matrix products, arithmetic and copies ran while one was open for 5% -> 8% of each run, Pallas kernels for 0% -> 0%
where the time goes in v1:
time: 566 us; the launch traced here: 558 us
  waiting for transfers between devices  384 us (68%)
  matrix products  73.1 us (13%)
  blocking collectives  42.2 us (7%)
  other arithmetic  33 us (6%)
  between operations  14.9 us (3%)
  local copies, waits for them, and re-layouts  9.13 us (2%)
    psum x1, waiting for transfers between devices, per_device(): lax.psum(tuple((part.astype(jnp.bfloat16) for part in (query_grad, key_gr...  101 us
    all_gather x1, waiting for transfers between devices, per_device(): normed_all = lax.all_gather(normed_own, 'tensor', axis=0, tiled=True)  45.8 us
    all_gather x1, waiting for transfers between devices, per_device(): second_all = lax.all_gather(second_own, 'tensor', axis=0, tiled=True)  44.6 us
    reduce_scatter x1, waiting for transfers between devices, per_device(): lax.psum_scatter((jnp.einsum('tf,cf->tc', left_back, left_weight, preferr...  42.7 us
    reduce_scatter x1, waiting for transfers between devices, per_device(): lax.psum_scatter(jnp.dot(gated, out_weight, preferred_element_type=jnp.fl...  42.7 us
    psum x1, blocking collectives, per_device(): lax.psum((first_part, second_part), ('dp', 'tensor'))  42.2 us
    all_gather x1, waiting for transfers between devices, per_device(): down_in = lax.all_gather(cotangent, 'tensor', axis=0, tiled=True)  37.5 us
    all_gather x1, waiting for transfers between devices, per_device(): lax.all_gather(resid_grad.astype(jnp.bfloat16), 'tensor', axis=0, tiled=T...  34.6 us
  transfers between devices with their start and end apart: 9, of which 9 were waited for; matrix products, arithmetic and copies ran while one was open for 8% of the time, Pallas kernels for 0%

profile of v1, /device:TPU:0, one launch (start us, length us, event | category | flops | bytes accessed | tf_op | source)
XLA Modules:
  0.0 557.5 jit_solution(13068382878314407634)
XLA Ops:
  14.3 45.8 %all-gather.5.cloned.1.call-done = bf16[1024,1024]{1,0:T(8,128)(2,1)} async-done(((bf16[256,1024]{1,0:T(8,128)(2,1)}), bf16[1024,1024]{1,0:T(8,128)(2,1)}) %all-gather.5.cloned.1.call-update) | async-done | bytes 2097168 | tf_op jit(solution)/shard_map/all_gather | solution.py:55
  60.1 4.7 fusion.40
  68.8 2.7 multiply_reduce_fusion.2
  76.4 42.7 %reduce-scatter.5.cloned.1.call-done = bf16[256,1024]{1,0:T(8,128)(2,1)} async-done(((bf16[1024,1024]{1,0:T(8,128)(2,1)}), bf16[256,1024]{1,0:T(8,128)(2,1)}) %reduce-scatter.5.cloned.1.call-update) | async-done | bytes 524304 | tf_op jit(solution)/shard_map/reduce_scatter | solution.py:77
  123.3 44.6 %all-gather.7.cloned.1.call-done = bf16[1024,1024]{1,0:T(8,128)(2,1)} async-done(((bf16[256,1024]{1,0:T(8,128)(2,1)}), bf16[1024,1024]{1,0:T(8,128)(2,1)}) %all-gather.7.cloned.1.call-update) | async-done | bytes 2097168 | tf_op jit(solution)/shard_map/all_gather | solution.py:86
  167.9 5.4 fusion.42
  173.3 3.3 fusion.41
  176.6 37.5 %all-gather.9.cloned.1.call-done = bf16[1024,1024]{1,0:T(8,128)(2,1)} async-done(((bf16[256,1024]{1,0:T(8,128)(2,1)}), bf16[1024,1024]{1,0:T(8,128)(2,1)}) %all-gather.9.cloned.1.call-update) | async-done | bytes 2097168 | tf_op jit(solution)/shard_map/all_gather | solution.py:98
  214.1 6.3 %multiply_convert_fusion = (bf16[1024,704]{0,1:T(8,128)(2,1)S(1)}, bf16[1024,704]{0,1:T(8,128)(2,1)}, bf16[1024,704]{0,1:T(8,128)(2,1)S(1)}) fusion(f32[1024,704]{0,1:T(8,128)} %fusion.41, f32[1024,704]{0,1:T(8,128)} %fusion.42, bf16[1024,1024]{1,0:T(8,128)(2,1)} %all-gather.9.cloned.1.call-done, bf16[704,1024]{1,0:T(8,128)(2,1)S(1)} %copy-done), kind=kOutput, calls=%fused_computation.7 | convolution fusion | flops 1480720384 | bytes 13631488 | tf_op jit(solution)/shard_map/td,fd->tf/dot_general | solution.py:100
  222.8 3.2 add_convert_fusion
  226.1 42.7 %reduce-scatter.9.cloned.1.call-done = bf16[256,1024]{1,0:T(8,128)(2,1)} async-done(((bf16[1024,1024]{1,0:T(8,128)(2,1)}), bf16[256,1024]{1,0:T(8,128)(2,1)}) %reduce-scatter.9.cloned.1.call-update) | async-done | bytes 524304 | tf_op jit(solution)/shard_map/reduce_scatter | solution.py:105
  274.2 4.9 convolution_convert_fusion.4
  279.2 2.8 convolution_convert_fusion.5
  282.0 2.8 convolution_convert_fusion.6
  284.7 34.6 %all-gather.11.cloned.1.call-done = bf16[1024,1024]{1,0:T(8,128)(2,1)} async-done(((bf16[256,1024]{1,0:T(8,128)(2,1)}), bf16[1024,1024]{1,0:T(8,128)(2,1)}) %all-gather.11.cloned.1.call-update) | async-done | bytes 2097168 | tf_op jit(solution)/shard_map/all_gather | solution.py:116
  319.3 4.1 fusion.38
  324.0 5.1 convolution_convert_fusion.7
  333.4 2.9 fusion.3
  342.9 5.6 %convolution_convert_fusion.1 = bf16[1024,1024]{1,0:T(8,128)(2,1)} fusion(bf16[1024,1024]{1,0:T(8,128)(2,1)} %copy-done.35, bf16[1024,256]{0,1:T(8,128)(2,1)} %copy-done.52, bf16[1024,256]{0,1:T(8,128)(2,1)S(1)} %bitcast.98, bf16[1024,256]{0,1:T(8,128)(2,1)S(1)} %bitcast.100, bf16[1024,256]{0,1:T(8,128)(2,1)} %bitcast.102), kind=kOutput, calls=%fused_computation.17 | convolution fusion | flops 2156920832 | bytes 6291456 | tf_op jit(solution)/shard_map/tq,cq->tc/dot_general | solution.py:160
  348.6 4.6 convolution_convert_fusion.3
  353.2 101.3 %all-reduce.4.cloned.1.call-done = (bf16[1024,256]{1,0:T(8,128)(2,1)}, bf16[1024,256]{1,0:T(8,128)(2,1)}, bf16[1024,256]{1,0:T(8,128)(2,1)}, bf16[1024,256]{1,0:...) async-done(((bf16[1024,256]{1,0:T(8,128)(2,1)}, bf16[1024,256]{1,0:T(8,128)(2,1)}, ...) | async-done | bytes 6946832 | tf_op jit(solution)/shard_map/psum | solution.py:173
  467.9 33.0 %reduce-scatter.11.cloned.1.call-done = bf16[256,1024]{1,0:T(8,128)(2,1)} async-done(((bf16[1024,1024]{1,0:T(8,128)(2,1)}), bf16[256,1024]{1,0:T(8,128)(2,1)}) %reduce-scatter.11.cloned.1.call-update) | async-done | bytes 524304 | tf_op jit(solution)/shard_map/reduce_scatter | solution.py:159
  502.9 42.2 %all-reduce = (f32[1024]{0:T(1024)}, f32[1024]{0:T(1024)}) all-reduce(f32[1024]{0:T(1024)} %get-tuple-element.14, f32[1024]{0:T(1024)S(1)} %copy-done.42), channel_id=1, replica_groups=mesh['dp'=8,'tensor'=4] {'dp','tensor'}, use_global_device_ids=true, to_apply=%region_19.20 | all-reduce | flops 2048 | bytes 16384 | tf_op jit(solution)/shard_map/psum | solution.py:190
  547.4 3.1 fusion.15
  (165 shorter events, 56.8 us)
Async XLA Ops:
  7.2 206.9 %copy-start = (bf16[704,1024]{1,0:T(8,128)(2,1)S(1)}, bf16[704,1024]{1,0:T(8,128)(2,1)}, u32[]{:S(2)}) copy-start(bf16[704,1024]{1,0:T(8,128)(2,1)} %param.22) | copy-start | bytes 4325380
  7.2 52.9 %all-gather.5.cloned.1.call-start = ((), (), s32[]{:S(2)}) async-start(), calls=%async_computation.4 | async-start | bytes 2621440 | tf_op jit(solution)/shard_map/all_gather | solution.py:55
  11.3 107.8 %reduce-scatter.5.cloned.1.call-start = ((), (), s32[]{:S(2)}) async-start(), calls=%async_computation.5 | async-start | bytes 2621440 | tf_op jit(solution)/shard_map/reduce_scatter | solution.py:77
  14.3 51.7 %copy-start.24 = (pred[1024,1024]{1,0:T(8,128)(4,1)}, pred[1024,1024]{1,0:T(8,128)(4,1)S(1)}, u32[]{:S(2)}) copy-start(pred[1024,1024]{1,0:T(8,128)(4,1)S(1)} %fusion) | copy-start | bytes 3145732
  64.8 7.4 %copy-start.12 = (f32[1024,1024]{0,1:T(8,128)}, f32[1024,1024]{0,1:T(8,128)S(1)}, u32[]{:S(2)}) copy-start(f32[1024,1024]{0,1:T(8,128)S(1)} %fusion.40) | copy-start | bytes 12582916
  74.3 44.8 %copy-start.2 = (bf16[256,1024]{1,0:T(8,128)(2,1)S(1)}, bf16[256,1024]{1,0:T(8,128)(2,1)}, u32[]{:S(2)}) copy-start(bf16[256,1024]{1,0:T(8,128)(2,1)} %param.13) | copy-start | bytes 1572868
  76.3 44.1 %copy-start.36 = (f32[1024]{0:T(1024)S(1)}, f32[1024]{0:T(1024)}, u32[]{:S(2)}) copy-start(f32[1024]{0:T(1024)} %param.24) | copy-start | bytes 12292
  76.4 91.5 %all-gather.7.cloned.1.call-start = ((), (), s32[]{:S(2)}) async-start(), calls=%async_computation.6 | async-start | bytes 2621440 | tf_op jit(solution)/shard_map/all_gather | solution.py:86
  120.4 52.9 %copy-start.39 = (f32[256]{0:T(256)}, f32[256]{0:T(256)S(1)}, u32[]{:S(2)}) copy-start(f32[256]{0:T(256)S(1)} %add_rsqrt_fusion.1) | copy-start | bytes 3076
  122.5 91.6 %all-gather.9.cloned.1.call-start = ((), (), s32[]{:S(2)}) async-start(), calls=%async_computation.8 | async-start | bytes 2621440 | tf_op jit(solution)/shard_map/all_gather | solution.py:98
  123.0 145.7 %reduce-scatter.9.cloned.1.call-start = ((), (), s32[]{:S(2)}) async-start(), calls=%async_computation.9 | async-start | bytes 2621440 | tf_op jit(solution)/shard_map/reduce_scatter | solution.py:105
  214.1 6.4 %copy-start.50 = (bf16[1024,704]{0,1:T(8,128)(2,1)S(1)}, bf16[1024,704]{0,1:T(8,128)(2,1)}, u32[]{:S(2)}) copy-start(bf16[1024,704]{0,1:T(8,128)(2,1)} %param.20) | copy-start | bytes 4325380
  226.0 42.8 %copy-start.3 = (bf16[256,1024]{1,0:T(8,128)(2,1)S(1)}, bf16[256,1024]{1,0:T(8,128)(2,1)}, u32[]{:S(2)}) copy-start(bf16[256,1024]{1,0:T(8,128)(2,1)} %reduce-scatter.5.cloned.1.call-done) | copy-start | bytes 1572868
  226.0 93.3 %all-gather.11.cloned.1.call-start = ((), (), s32[]{:S(2)}) async-start(), calls=%async_computation.10 | async-start | bytes 2621440 | tf_op jit(solution)/shard_map/all_gather | solution.py:116
  273.9 180.6 %all-reduce.4.cloned.1.call-start = ((), (), s32[]{:S(2)}) async-start(), calls=%async_computation.12 | async-start | bytes 13893632 | tf_op jit(solution)/shard_map/psum | solution.py:173
  323.4 12.9 %copy-start.52 = (bf16[1024,256]{0,1:T(8,128)(2,1)}, bf16[1024,256]{0,1:T(8,128)(2,1)S(1)}, u32[]{:S(2)}) copy-start(bf16[1024,256]{0,1:T(8,128)(2,1)S(1)} %get-tuple-element.27) | copy-start | bytes 1572868
  342.8 158.1 %reduce-scatter.11.cloned.1.call-start = ((), (), s32[]{:S(2)}) async-start(), calls=%async_computation.11 | async-start | bytes 2621440 | tf_op jit(solution)/shard_map/reduce_scatter | solution.py:159
  348.5 198.9 %reduce-scatter.7.cloned.1.call-start = ((), (), s32[]{:S(2)}) async-start(), calls=%async_computation.7 | async-start | bytes 2621440 | tf_op jit(solution)/shard_map/reduce_scatter | solution.py:90
  465.9 35.0 %copy-start.38 = (f32[1024]{0:T(1024)S(1)}, f32[1024]{0:T(1024)}, u32[]{:S(2)}) copy-start(f32[1024]{0:T(1024)} %param.23) | copy-start | bytes 12292
  465.9 36.9 %copy-start.42 = (f32[1024]{0:T(1024)S(1)}, f32[1024]{0:T(1024)}, u32[]{:S(2)}) copy-start(f32[1024]{0:T(1024)} %get-tuple-element.12) | copy-start | bytes 12292
  465.9 81.5 %copy-start.5 = (bf16[256,1024]{1,0:T(8,128)(2,1)S(1)}, bf16[256,1024]{1,0:T(8,128)(2,1)}, u32[]{:S(2)}) copy-start(bf16[256,1024]{1,0:T(8,128)(2,1)} %param.25) | copy-start | bytes 1572868
  465.9 81.5 %copy-start.6 = (bf16[256,1024]{1,0:T(8,128)(2,1)S(1)}, bf16[256,1024]{1,0:T(8,128)(2,1)}, u32[]{:S(2)}) copy-start(bf16[256,1024]{1,0:T(8,128)(2,1)} %reduce-scatter.9.cloned.1.call-done) | copy-start | bytes 1572868
  466.0 81.5 %copy-start.37 = (f32[1024]{0:T(1024)S(1)}, f32[1024]{0:T(1024)}, u32[]{:S(2)}) copy-start(f32[1024]{0:T(1024)} %param.24) | copy-start | bytes 12292
  466.0 81.5 %copy-start.40 = (f32[256]{0:T(256)S(1)}, f32[256]{0:T(256)}, u32[]{:S(2)}) copy-start(f32[256]{0:T(256)} %copy-done.39) | copy-start | bytes 3076
  (38 other events, 112.6 us)
Sparse Core Ops, SparseCore 0:
  11.4 48.6 all-gather.4
  76.5 42.5 reduce-scatter.4
  122.6 45.2 all-gather.6
  169.4 44.6 all-gather.8
  226.2 42.5 reduce-scatter.8
  274.0 45.2 all-gather.10
  342.9 111.5 all-reduce.3
  456.9 43.9 reduce-scatter.10
  503.2 44.1 reduce-scatter.6

commit v2 on v0

v2 whole, which is shorter than its diff:
```python
import functools

import jax
import jax.numpy as jnp
from jax import lax
from jax.experimental import pallas as pl
from jax.experimental.pallas import tpu as pltpu
from jax.sharding import PartitionSpec as P

EPS = 1e-05
HEAD = 64
BF = jnp.bfloat16
F32 = jnp.float32
MESH = pl.DeviceIdType.MESH
ANY = pl.BlockSpec(memory_space=pl.ANY)
INNER = pl.BlockSpec(memory_space=pltpu.VMEM)
PIECE_BITS = 3


def dot(a, b):
    return lax.dot_general(a, b, (((1,), (0,)), ((), ())), preferred_element_type=F32)


def dot_t(a, b):
    return lax.dot_general(a, b, (((1,), (1,)), ((), ())), preferred_element_type=F32)


class Place:
    def __init__(self, dp_size):
        self.i = lax.axis_index("dp")
        self.t = lax.axis_index("tensor")
        self.half = lax.rem(self.t, 2)
        self.pair = self.t // 2
        self.bits = dp_size.bit_length() - 1
        self.mate = {"tensor": self.t + 1 - 2 * self.half}
        self.twin = {"tensor": self.t + 2 - 4 * self.pair}

    def bit(self, b):
        return lax.rem(self.i // (1 << b), 2)

    def over(self, b):
        return {"dp": self.i + (1 << b) * (1 - 2 * self.bit(b))}

    def greet(self):
        barrier = pltpu.get_barrier_semaphore()
        peers = [self.mate, self.twin] + [self.over(b) for b in range(self.bits)]
        for peer in peers:
            pl.semaphore_signal(barrier, inc=1, device_id=peer, device_id_type=MESH)
        pl.semaphore_wait(barrier, len(peers))


class Links:
    def __init__(self, send_sem, recv_sem):
        self.send_sem, self.recv_sem, self.count, self.open = send_sem, recv_sem, 0, []

    def start(self, source, target, peer):
        copy = pltpu.make_async_remote_copy(
            src_ref=source,
            dst_ref=target,
            send_sem=self.send_sem.at[self.count],
            recv_sem=self.recv_sem.at[self.count],
            device_id=peer,
            device_id_type=MESH,
        )
        self.count += 1
        copy.start()
        self.open.append(copy)
        return copy

    def finish(self):
        for copy in self.open:
            copy.wait_send()


class Moves:
    def __init__(self, sem):
        self.sem, self.count, self.open = sem, 0, []

    def start(self, source, target):
        copy = pltpu.make_async_copy(source, target, self.sem.at[self.count])
        self.count += 1
        copy.start()
        self.open.append(copy)
        return copy

    def wait(self, copy):
        copy.wait()
        self.open = [other for other in self.open if other is not copy]

    def finish(self):
        for copy in list(self.open):
            self.wait(copy)


def part(ref, lead, axis, first, count):
    window = pl.ds(first, count)
    return ref.at[lead + ((window, slice(None)) if axis == 0 else (slice(None), window))]


def piece_of(place, order):
    total = 0
    for b in order:
        total = 2 * total + place.bit(b)
    return total


class Gather:
    def __init__(self, place, links, ref, lead, axis, order):
        self.place, self.links, self.ref, self.lead, self.axis, self.order = place, links, ref, lead, axis, order
        self.size = ref.shape[len(ref.shape) - 2 + axis] // (1 << len(order))
        self.piece = piece_of(place, order)
        self.copy, self.stage = None, 0

    def block(self, shard, width):
        first = (self.piece // width) * (width * self.size)
        return part(self.ref, (shard,) + self.lead, self.axis, pl.multiple_of(first, self.size), width * self.size)

    def begin(self):
        self.copy = self.links.start(self.block(0, 1), self.block(1, 1), self.place.twin)

    def advance(self):
        self.copy.wait_recv()
        if self.stage < len(self.order):
            block = self.block(1, 1 << self.stage)
            self.copy = self.links.start(block, block, self.place.over(self.order[-1 - self.stage]))
        self.stage += 1

    def complete(self):
        while self.stage <= len(self.order):
            self.advance()


def rows_loop(count, size, body):
    def step(k, carry):
        body(pl.multiple_of(k * size, size))
        return carry

    lax.fori_loop(0, count // size, step, 0)


def softplus_and_slope(values):
    tail = jnp.exp(-jnp.abs(values))
    soft = jnp.maximum(values, 0.0) + jnp.log1p(tail)
    slope = jnp.where(values >= 0, 1.0, tail) / (1.0 + tail)
    return soft, slope


def sigmoid(values):
    tail = jnp.exp(-jnp.abs(values))
    return jnp.where(values >= 0, 1.0, tail) / (1.0 + tail)


def head_of(shape, axis):
    return lax.broadcasted_iota(jnp.int32, shape, axis) // HEAD


def same_head(width):
    return head_of((width, width), 0) == head_of((width, width), 1)


def head_mean(values):
    ones = jnp.where(same_head(values.shape[-1]), 1.0 / HEAD, 0.0).astype(BF)
    return dot(values.astype(BF), ones)


def fold(state):
    width = state.shape[-1]
    state = jnp.where(same_head(width), state, 0.0)
    return (state[:, : width // 2] + state[:, width // 2 :]).astype(BF)


def unfold(state):
    both = jnp.concatenate((state, state), axis=1)
    return jnp.where(same_head(both.shape[-1]), both, jnp.zeros_like(both))


def only_head(values, head):
    return jnp.where(head_of(values.shape, 1) == head, values, jnp.zeros_like(values))


def near_marks(place, segc_ref, tokens):
    own = segc_ref[pl.ds(pl.multiple_of(place.pair * tokens, tokens), tokens), :]
    return own == segc_ref[tokens - 1 : tokens, :]


def doc_mask(place, segr_ref, segc_ref, mask_ref, tokens, later):
    offset = pl.multiple_of(place.pair * tokens, tokens)
    across = segr_ref[:, pl.ds(offset, tokens)]

    def body(first):
        down = segc_ref[pl.ds(pl.multiple_of(offset + first, 64), 64), :]
        at = first + lax.broadcasted_iota(jnp.int32, (64, tokens), 0)
        col = lax.broadcasted_iota(jnp.int32, (64, tokens), 1)
        order = col >= at if later else col <= at
        mask_ref[pl.ds(first, 64), :] = jnp.where((down == across) & order, 1.0, 0.0).astype(BF)

    rows_loop(tokens, 64, body)


def forward_kernel(
    dp_size,
    x_hbm, segr_ref, segc_ref, wq, wk, wv, wz, wo, wl, wr, wd, g1_ref, g2_ref, cot_hbm,
    normed_t_out, second_t_out, gated_t_out, product_t_out, dleft_out, dright_out, cot_out,
    qp_out, kp_out, vl_out, sq_out, sk_out, hn_out, rr_out, sz_out, state_out,
    joined_out, ow_out, dres_out, block_out, gain_out,
    x_ref, normed, normed_t, joined, ow, lw, rw, dw, qp, kp, vl, sq, sk, hn, rr, sz, gated, gated_t, mask,
    state_send, state_recv, branch_send, branch_recv, resid, own_sum, second, second_t, cot,
    product, product_t, dleft, dright, ffn_send, ffn_recv, ffn_own, back_send, back_recv, dres, blk, gain,
    send_sem, recv_sem, move_sem,
):
    place = Place(dp_size)
    links, moves = Links(send_sem, recv_sem), Moves(move_sem)
    own, width = x_ref.shape
    tokens = 2 * own
    mine = pl.multiple_of(place.half * own, own)
    theirs = pl.multiple_of((1 - place.half) * own, own)

    x_in = moves.start(x_hbm, x_ref)
    joined_in = [moves.start(w, joined.at[0, j]) for j, w in enumerate((wq, wk, wv, wz))]
    ow_in = moves.start(wo, ow.at[0])
    ffn_in = [moves.start(w, v.at[0]) for w, v in ((wl, lw), (wr, rw), (wd, dw))]
    cot_in = moves.start(cot_hbm, cot.at[pl.ds(mine, own), :])
    place.greet()

    def norm(first, source, gain_row):
        values = source[pl.ds(first, 32), :].astype(F32)
        scale = lax.rsqrt(jnp.mean(values * values, axis=-1, keepdims=True) + EPS)
        return values, scale, values * scale * gain_row

    moves.wait(x_in)

    def first_norm(first):
        normed[pl.ds(mine + first, 32), :] = norm(first, x_ref, g1_ref[...])[2].astype(BF)

    rows_loop(own, 32, first_norm)
    block = normed.at[pl.ds(mine, own), :]
    normed_copy = links.start(block, block, place.mate)

    first_order, second_order = (0, 1, 2), (0, 2, 1)
    gather_joined = [
        Gather(place, links, joined, (pl.ds(0, 2),), 0, first_order),
        Gather(place, links, joined, (pl.ds(2, 2),), 0, second_order),
    ]
    gather_ow = Gather(place, links, ow, (), 0, second_order)
    gather_ffn = [
        Gather(place, links, lw, (), 0, first_order),
        Gather(place, links, rw, (), 0, second_order),
        Gather(place, links, dw, (), 1, first_order),
    ]
    for copy in joined_in:
        moves.wait(copy)
    for unit in gather_joined:
        unit.begin()
    moves.wait(ow_in)
    gather_ow.begin()
    attn_units = gather_joined + [gather_ow]

    def project(shard, first):
        rows = normed[pl.ds(first, own), :]
        at = pl.ds(first, own)
        soft, slope = softplus_and_slope(dot(rows, joined[shard, 0]))
        qp[shard, at, :] = soft.astype(BF)
        sq[shard, at, :] = slope.astype(BF)
        soft, slope = softplus_and_slope(dot(rows, joined[shard, 1]))
        kp[shard, at, :] = soft.astype(BF)
        sk[shard, at, :] = slope.astype(BF)
        vl[shard, at, :] = dot(rows, joined[shard, 2]).astype(BF)
        sz[shard, at, :] = sigmoid(dot(rows, joined[shard, 3]))

    project(0, mine)
    doc_mask(place, segr_ref, segc_ref, mask, tokens, False)
    for unit in attn_units:
        unit.advance()
    for copy in ffn_in:
        moves.wait(copy)
    normed_copy.wait_recv()
    for unit in gather_ffn:
        unit.begin()
    moves.wait(cot_in)
    cot_block = cot.at[pl.ds(mine, own), :]
    cot_copy = links.start(cot_block, cot_block, place.mate)

    project(0, theirs)
    near = near_marks(place, segc_ref, tokens)
    state_copy = [None, None]

    def send_state(shard):
        keys = jnp.where(near, kp[shard].astype(F32), 0.0).astype(BF)
        state_send[shard] = fold(dot(keys.T, vl[shard]))
        state_copy[shard] = links.start(state_send.at[shard], state_recv.at[1 - shard], place.twin)

    def mix(shard):
        def one(head, carry):
            for r in range(2):
                seen = (r + 1) * own
                at = slice(r * own, (r + 1) * own)
                query = only_head(qp[shard, at, :], head)
                raw = dot_t(query, kp[shard, :seen, :])
                scores = raw.astype(BF) * mask[at, :seen]
                hn[shard, at, :] += dot(scores, only_head(vl[shard, :seen, :], head))
            return carry

        hn[shard] = jnp.zeros(hn.shape[1:], F32)
        lax.fori_loop(0, hn.shape[-1] // HEAD, one, 0)

    send_state(0)
    for unit in attn_units:
        unit.advance()
    mix(0)
    for unit in attn_units:
        unit.advance()
    for unit in gather_ffn:
        unit.advance()
    for unit in attn_units:
        unit.complete()
    project(1, mine)
    project(1, theirs)
    send_state(1)
    for unit in gather_ffn:
        unit.advance()
    mix(1)
    for unit in gather_ffn:
        unit.advance()

    second_half = place.pair == 1

    def open_gate(shard):
        state_copy[1 - shard].wait_recv()
        marks = near & second_half
        query = jnp.where(marks, qp[shard].astype(F32), 0.0).astype(BF)
        mixed = hn[shard] + dot(query, unfold(state_recv[shard]))
        scale = lax.rsqrt(head_mean(mixed * mixed) + EPS)
        rr[shard] = scale
        hn[shard] = mixed * scale
        gated[shard] = (mixed * scale * sz[shard]).astype(BF)

    open_gate(0)
    open_gate(1)

    def branch(first):
        at = pl.ds(first, own)
        return dot(gated[0, at, :], ow[0]) + dot(gated[1, at, :], ow[1])

    branch_send[...] = branch(theirs).astype(BF)
    branch_copy = links.start(branch_send, branch_recv, place.mate)
    own_sum[...] = branch(mine)
    for shard in range(2):
        gated_t[shard] = gated[shard].T
    for unit in gather_ffn:
        unit.complete()
    outs = [
        (joined.at[1], joined_out), (ow.at[1], ow_out), (qp, qp_out), (kp, kp_out), (vl, vl_out), (sq, sq_out),
        (sk, sk_out), (hn, hn_out), (rr, rr_out), (sz, sz_out), (state_recv, state_out), (gated_t, gated_t_out),
    ]
    for source, target in outs:
        moves.start(source, target)
    branch_copy.wait_recv()

    def second_norm(first):
        at = pl.ds(first, 32)
        values = x_ref[at, :].astype(F32) + own_sum[at, :] + branch_recv[at, :].astype(F32)
        resid[at, :] = values
        scale = lax.rsqrt(jnp.mean(values * values, axis=-1, keepdims=True) + EPS)
        second[pl.ds(mine + first, 32), :] = (values * scale * g2_ref[...]).astype(BF)

    rows_loop(own, 32, second_norm)
    block = second.at[pl.ds(mine, own), :]
    second_copy = links.start(block, block, place.mate)
    cot_copy.wait_recv()
    moves.start(cot, cot_out)

    def unit_rows(first):
        at = pl.ds(first, own)

        def one(shard, carry):
            left = dot(second[at, :], lw[shard])
            right = dot(second[at, :], rw[shard])
            product[shard, at, :] = (left * right).astype(BF)
            grad = dot_t(cot[at, :], dw[shard])
            dleft[shard, at, :] = (grad * right).astype(BF)
            dright[shard, at, :] = (grad * left).astype(BF)
            return carry

        lax.fori_loop(0, 2, one, 0)

    unit_rows(mine)
    for c in range(0, width, 256):
        normed_t[c : c + 256, :] = normed[:, c : c + 256].T
    moves.start(normed_t, normed_t_out)
    second_copy.wait_recv()
    unit_rows(theirs)

    def back(first):
        at = pl.ds(first, own)
        return (
            dot_t(dleft[0, at, :], lw[0])
            + dot_t(dright[0, at, :], rw[0])
            + dot_t(dleft[1, at, :], lw[1])
            + dot_t(dright[1, at, :], rw[1])
        )

    def ffn(first):
        at = pl.ds(first, own)
        return dot(product[0, at, :], dw[0]) + dot(product[1, at, :], dw[1])

    back_send[...] = back(theirs).astype(BF)
    back_copy = links.start(back_send, back_recv, place.mate)
    moves.start(dleft, dleft_out)
    moves.start(dright, dright_out)
    ffn_send[...] = ffn(theirs).astype(BF)
    ffn_copy = links.start(ffn_send, ffn_recv, place.mate)
    own_sum[...] = back(mine)
    ffn_own[...] = ffn(mine)
    for c in range(0, width, 256):
        second_t[c : c + 256, :] = second[:, c : c + 256].T
    moves.start(second_t, second_t_out)
    for shard in range(2):
        product_t[shard] = product[shard].T
    moves.start(product_t, product_t_out)
    gain[...] = jnp.zeros(gain.shape, F32)
    back_copy.wait_recv()

    def residual_back(first):
        at = pl.ds(first, 32)
        values = resid[at, :]
        scale = lax.rsqrt(jnp.mean(values * values, axis=-1, keepdims=True) + EPS)
        grad = own_sum[at, :] + back_recv[at, :].astype(F32)
        gain[0:1, :] += jnp.sum(grad * values * scale, axis=0, keepdims=True)
        weighted = grad * g2_ref[...]
        inner = jnp.mean(weighted * values, axis=-1, keepdims=True)
        upstream = cot[pl.ds(mine + first, 32), :].astype(F32)
        dres[at, :] = upstream + scale * weighted - values * (scale * scale * scale * inner)

    rows_loop(own, 32, residual_back)
    moves.start(dres, dres_out)
    moves.start(gain, gain_out)
    ffn_copy.wait_recv()

    def finish_block(first):
        at = pl.ds(first, 32)
        blk[at, :] = (resid[at, :] + ffn_own[at, :] + ffn_recv[at, :].astype(F32)).astype(BF)

    rows_loop(own, 32, finish_block)
    moves.start(blk, block_out)
    moves.finish()
    links.finish()


class Reduce:
    def __init__(self, place, links, moves, grad, axis, order, halves, extra, twin_recv, done, out):
        self.place, self.links, self.moves = place, links, moves
        self.grad, self.axis, self.order = grad, axis, order
        self.halves, self.extra, self.twin_recv, self.done, self.out = halves, extra, twin_recv, done, out
        self.size = grad.shape[1 + axis] // (1 << len(order))
        self.piece = piece_of(place, order)
        self.stage, self.copy, self.local = 0, None, None
        self.steps = len(order) + len(extra) + 1 + len(order)

    def first_of(self, width):
        return pl.multiple_of((self.piece // width) * (width * self.size), self.size)

    def grad_part(self, lead, first, width):
        return part(self.grad, lead, self.axis, pl.multiple_of(first, self.size), width * self.size)

    def out_part(self, width):
        return part(self.out, (), self.axis, self.first_of(width), width * self.size)

    def begin(self):
        shards, folds = (slice(None),), len(self.order)
        k = self.stage
        if k < folds:
            width = 1 << (folds - 1 - k)
            bit = self.place.bit(self.order[k])
            away = self.first_of(width) + (1 - 2 * bit) * (width * self.size)
            self.copy = self.links.start(
                self.grad_part(shards, away, width), self.halves[k], self.place.over(self.order[k])
            )
            return
        k -= folds
        if k < len(self.extra):
            source = self.grad_part(shards, self.first_of(1), 1)
            self.copy = self.links.start(source, self.extra[k], self.place.over(folds + k))
            return
        k -= len(self.extra)
        if k == 0:
            source = self.grad_part((1,), self.first_of(1), 1)
            self.copy = self.links.start(source, self.twin_recv, self.place.twin)
            return
        k -= 1
        block = self.out_part(1 << k)
        source = self.done if k == 0 else block
        self.copy = self.links.start(source, block, self.place.over(self.order[folds - 1 - k]))
        if k == 0:
            self.local = self.moves.start(self.done, block)

    def add(self, recv, width, target=None):
        rows = recv.shape[-2]
        chunk = 32
        first = self.first_of(width)
        shards = 1 if target is not None else 2

        def body(at):
            for shard in range(shards):
                lead = (shard,)
                if self.axis == 0:
                    where = lead + (pl.ds(pl.multiple_of(first + at, chunk), chunk), slice(None))
                else:
                    where = lead + (pl.ds(at, chunk), pl.ds(first, width * self.size))
                if target is None:
                    self.grad[where] = self.grad[where] + recv[shard, pl.ds(at, chunk), :]
                else:
                    target[pl.ds(at, chunk), :] = self.grad[where] + recv[pl.ds(at, chunk), :]

        rows_loop(rows, chunk, body)

    def advance(self):
        if self.stage >= self.steps:
            return
        folds = len(self.order)
        self.copy.wait_recv()
        k = self.stage
        if k < folds:
            self.add(self.halves[k], 1 << (folds - 1 - k))
        elif k < folds + len(self.extra):
            self.copy.wait_send()
            self.links.open = [other for other in self.links.open if other is not self.copy]
            self.add(self.extra[k - folds], 1)
        elif k == folds + len(self.extra):
            self.add(self.twin_recv, 1, self.done)
        elif self.local is not None:
            self.moves.wait(self.local)
            self.local = None
        self.stage += 1
        if self.stage < self.steps:
            self.begin()

    def over(self):
        return self.stage >= self.steps


def backward_kernel(
    dp_size, extras, unit_shapes,
    normed_t_in, second_t_in, gated_t_in, product_t_in, dleft_in, dright_in, cot_in,
    qp_in, kp_in, vl_in, sq_in, sk_in, hn_in, rr_in, sz_in, state_in,
    wq, wk, wv, wz, joined_in, wo, ow_in, dres_in, gain_in, x_hbm, segr_ref, segc_ref, g1_ref,
    *rest,
):
    count = len(unit_shapes)
    outs, rest = rest[:count], rest[count:]
    block_out, gains_out = rest[:2]
    rest = rest[2:]
    grads, rest = rest[:count], rest[count:]
    received, rest = rest[: count * (PIECE_BITS + extras + 2)], rest[count * (PIECE_BITS + extras + 2) :]
    (
        second_t, gated_t, product_t, dleft, dright, cot, qp, kp, vl, sq, sk, hn, rr, sz, state,
        joined, ow, dres, gains, gains_recv, x_ref, dres_all, dm, djoined, mask, mask_t,
        dq, dk, dv, meet_send, meet_recv, back_send, back_recv, own_sum, blk,
        send_sem, recv_sem, move_sem,
    ) = rest
    place = Place(dp_size)
    links, moves = Links(send_sem, recv_sem), Moves(move_sem)
    own, width = x_ref.shape
    tokens = 2 * own
    mine = pl.multiple_of(place.half * own, own)
    theirs = pl.multiple_of((1 - place.half) * own, own)

    loads = {}
    for name, source, target in (
        ("dres", dres_in, dres), ("product", product_t_in, product_t), ("cot", cot_in, cot),
        ("second", second_t_in, second_t), ("left", dleft_in, dleft), ("right", dright_in, dright),
        ("ow0", wo, ow.at[0]), ("ow1", ow_in, ow.at[1]), ("sz", sz_in, sz), ("hn", hn_in, hn), ("rr", rr_in, rr),
        ("gated", gated_t_in, gated_t), ("qp", qp_in, qp), ("kp", kp_in, kp),
        ("vl", vl_in, vl), ("sq", sq_in, sq), ("sk", sk_in, sk), ("state", state_in, state),
        ("j0", wq, joined.at[0, 0]), ("j1", wk, joined.at[0, 1]), ("j2", wv, joined.at[0, 2]),
        ("j3", wz, joined.at[0, 3]), ("joined", joined_in, joined.at[1]), ("x", x_hbm, x_ref),
        ("gain", gain_in, gains.at[0]),
    ):
        loads[name] = moves.start(source, target)

    def ready(*names):
        for name in names:
            moves.wait(loads[name])

    place.greet()
    ready("dres")

    def round_dres(first):
        dres_all[pl.ds(mine + first, 32), :] = dres[pl.ds(first, 32), :].astype(BF)

    rows_loop(own, 32, round_dres)
    block = dres_all.at[pl.ds(mine, own), :]
    dres_copy = links.start(block, block, place.mate)

    per_unit = PIECE_BITS + extras + 2
    units = []
    for n, (_, axis, order) in enumerate(unit_shapes):
        bufs = received[n * per_unit : (n + 1) * per_unit]
        units.append(
            Reduce(
                place, links, moves, grads[n], axis, order, bufs[:PIECE_BITS],
                bufs[PIECE_BITS : PIECE_BITS + extras], bufs[-2], bufs[-1], outs[n],
            )
        )
    down_unit, left_unit, right_unit, ow_unit, q_unit, k_unit, v_unit, z_unit = units
    live = []

    def launch(unit):
        unit.begin()
        live.append(unit)

    def step_all():
        for unit in live:
            unit.advance()

    def outer(unit, left_of, right_of, chunk):
        rows = unit.grad.shape[1]

        def body(first):
            def one(shard, carry):
                unit.grad[shard, pl.ds(first, chunk), :] = dot(left_of(shard, first), right_of(shard)).astype(BF)
                return carry

            lax.fori_loop(0, 2, one, 0)

        rows_loop(rows, chunk, body)
        launch(unit)

    ready("product", "cot")
    down_chunk = product_t.shape[1] // 2
    outer(down_unit, lambda g, f: product_t[g, pl.ds(f, down_chunk), :], lambda g: cot[...], down_chunk)
    ready("second", "left")
    outer(left_unit, lambda g, f: second_t[pl.ds(f, 256), :], lambda g: dleft[g], 256)
    ready("right")
    outer(right_unit, lambda g, f: second_t[pl.ds(f, 256), :], lambda g: dright[g], 256)
    normed_t = second_t
    loads["normed"] = moves.start(normed_t_in, normed_t)
    doc_mask(place, segr_ref, segc_ref, mask, tokens, False)
    doc_mask(place, segr_ref, segc_ref, mask_t, tokens, True)
    near = near_marks(place, segc_ref, tokens)
    ready("ow0", "ow1", "sz", "hn", "rr", "qp")
    dres_copy.wait_recv()

    def gate_back(shard, carry):
        grad = dot_t(dres_all[...], ow[shard])
        opened, norm = sz[shard], hn[shard]
        djoined[shard, 3] = (grad * norm * opened * (1.0 - opened)).astype(BF)
        inner = grad * opened
        dm[shard] = (rr[shard] * (inner - norm * head_mean(inner * norm))).astype(BF)
        return carry

    lax.fori_loop(0, 2, gate_back, 0)
    meets = []
    for shard in range(2):
        query = jnp.where(near, qp[shard].astype(F32), 0.0).astype(BF)
        meet_send[shard] = fold(dot(query.T, dm[shard]))
        meets.append(links.start(meet_send.at[shard], meet_recv.at[1 - shard], place.twin))
    ready("gated", "normed")
    outer(ow_unit, lambda g, f: gated_t[g, pl.ds(f, 256), :], lambda g: dres_all[...], 256)

    def project_back(unit, j):
        outer(unit, lambda g, f: normed_t[pl.ds(f, 256), :], lambda g: djoined[g, j], 256)

    project_back(z_unit, 3)
    step_all()
    ready("kp", "vl", "sq", "sk", "state")
    first_half, second_half = place.pair == 0, place.pair == 1

    def mix_back(shard):
        dq[...] = jnp.where(near & second_half, dot_t(dm[shard], unfold(state[shard])), 0.0)
        dk[...] = jnp.zeros(dk.shape, F32)
        dv[...] = jnp.zeros(dv.shape, F32)

        def one(head, carry):
            for r in range(2):
                seen = (r + 1) * own
                at = slice(r * own, (r + 1) * own)
                grad_r, query_r = dm[shard, at, :], qp[shard, at, :]
                grad_h, query_h = only_head(grad_r, head), only_head(query_r, head)
                keys_h = only_head(kp[shard, :seen, :], head)
                vals_h = only_head(vl[shard, :seen, :], head)
                ds = dot_t(grad_r, vals_h).astype(BF) * mask[at, :seen]
                dq[at, :] += dot(ds, keys_h)
                st = dot_t(keys_h, query_r).astype(BF) * mask_t[:seen, at]
                dv[:seen, :] += dot(st, grad_h)
                dst = dot_t(vals_h, grad_r).astype(BF) * mask_t[:seen, at]
                dk[:seen, :] += dot(dst, query_h)
            return carry

        lax.fori_loop(0, dq.shape[-1] // HEAD, one, 0)

    for shard in range(2):
        mix_back(shard)
        if shard == 0:
            step_all()
        meets[1 - shard].wait_recv()
        meet = unfold(meet_recv[shard])
        marks = near & first_half
        djoined[shard, 2] = (dv[...] + jnp.where(marks, dot(kp[shard], meet), 0.0)).astype(BF)
        from_meet = jnp.where(marks, dot_t(vl[shard], meet), 0.0)
        djoined[shard, 1] = ((dk[...] + from_meet) * sk[shard].astype(F32)).astype(BF)
        djoined[shard, 0] = (dq[...] * sq[shard].astype(F32)).astype(BF)

    step_all()
    ready("j0", "j1", "j2", "j3", "joined")

    def normed_back(first):
        at = pl.ds(first, own)
        own_sum[...] = jnp.zeros(own_sum.shape, F32)

        def one(k, carry):
            own_sum[...] += dot_t(djoined[k // 4, lax.rem(k, 4), at, :], joined[k // 4, lax.rem(k, 4)])
            return carry

        lax.fori_loop(0, 8, one, 0)

    project_back(q_unit, 0)
    project_back(k_unit, 1)
    project_back(v_unit, 2)
    step_all()
    normed_back(theirs)
    back_send[...] = own_sum[...].astype(BF)
    back_copy = links.start(back_send, back_recv, place.mate)
    step_all()
    normed_back(mine)
    ready("x", "gain")
    step_all()
    back_copy.wait_recv()

    def finish_block(first):
        at = pl.ds(first, 32)
        values = x_ref[at, :].astype(F32)
        scale = lax.rsqrt(jnp.mean(values * values, axis=-1, keepdims=True) + EPS)
        grad = own_sum[at, :] + back_recv[at, :].astype(F32)
        gains[0, 1:2, :] += jnp.sum(grad * values * scale, axis=0, keepdims=True)
        weighted = grad * g1_ref[...]
        inner = jnp.mean(weighted * values, axis=-1, keepdims=True)
        blk[at, :] = (dres[at, :] + scale * weighted - values * (scale * scale * scale * inner)).astype(BF)

    rows_loop(own, 32, finish_block)
    moves.start(blk, block_out)

    peers = [place.over(b) for b in range(place.bits)] + [place.mate, place.twin]
    for n, peer in enumerate(peers):
        copy = links.start(gains.at[n], gains_recv.at[n], peer)
        step_all()
        copy.wait_recv()
        gains[n + 1] = gains[n] + gains_recv[n]
    moves.start(gains.at[len(peers)], gains_out)
    while not all(unit.over() for unit in live):
        step_all()
    moves.finish()
    links.finish()


def vmem(shape, dtype=BF):
    return pltpu.VMEM(shape, dtype)


def per_device(
    dp_size,
    inputs, segments, query_weight, key_weight, value_weight, gate_weight, out_weight, left_weight, right_weight,
    down_weight, norm_first, norm_second, cotangent,
):
    own, width = inputs.shape
    tokens = 2 * own
    local = query_weight.shape[1]
    hidden = left_weight.shape[1]
    bits = dp_size.bit_length() - 1
    extras = bits - PIECE_BITS
    shape = jax.ShapeDtypeStruct
    heads = (2, tokens, local)
    segr, segc = segments, segments.reshape(-1, 1)
    gain_one, gain_two = norm_first.reshape(1, -1), norm_second.reshape(1, -1)
    saved = [
        shape((width, tokens), BF), shape((width, tokens), BF), shape((2, local, tokens), BF),
        shape((2, hidden, tokens), BF), shape((2, tokens, hidden), BF), shape((2, tokens, hidden), BF),
        shape((tokens, width), BF), shape(heads, BF), shape(heads, BF), shape(heads, BF), shape(heads, BF),
        shape(heads, BF), shape(heads, F32), shape(heads, F32), shape(heads, F32), shape((2, local, local // 2), BF),
    ]
    results = pl.pallas_call(
        functools.partial(forward_kernel, dp_size),
        out_shape=saved
        + [
            shape((4, width, local), BF), shape((local, width), BF), shape((own, width), F32),
            shape((own, width), BF), shape((8, width), F32),
        ],
        in_specs=[ANY, INNER, INNER] + [ANY] * 8 + [INNER, INNER, ANY],
        out_specs=[ANY] * 21,
        scratch_shapes=[
            vmem((own, width)), vmem((tokens, width)), vmem((width, tokens)), vmem((2, 4, width, local)),
            vmem((2, local, width)), vmem((2, width, hidden)), vmem((2, width, hidden)), vmem((2, hidden, width)),
            vmem(heads), vmem(heads), vmem(heads), vmem(heads), vmem(heads), vmem(heads, F32), vmem(heads, F32),
            vmem(heads, F32), vmem(heads), vmem((2, local, tokens)), vmem((tokens, tokens)),
            vmem((2, local, local // 2)), vmem((2, local, local // 2)), vmem((own, width)), vmem((own, width)),
            vmem((own, width), F32), vmem((own, width), F32), vmem((tokens, width)), vmem((width, tokens)),
            vmem((tokens, width)), vmem((2, tokens, hidden)), vmem((2, hidden, tokens)), vmem((2, tokens, hidden)),
            vmem((2, tokens, hidden)), vmem((own, width)), vmem((own, width)), vmem((own, width), F32),
            vmem((own, width)), vmem((own, width)), vmem((own, width), F32), vmem((own, width)),
            vmem((8, width), F32),
            pltpu.SemaphoreType.DMA((40,)), pltpu.SemaphoreType.DMA((40,)), pltpu.SemaphoreType.DMA((40,)),
        ],
        compiler_params=pltpu.CompilerParams(collective_id=0, has_side_effects=True, vmem_limit_bytes=60 << 20),
    )(
        inputs, segr, segc, query_weight, key_weight, value_weight, gate_weight, out_weight, left_weight,
        right_weight, down_weight, gain_one, gain_two, cotangent,
    )
    kept, (joined, ow, dres, block, gain) = results[:16], results[16:]

    first_order, second_order = (0, 1, 2), (0, 2, 1)
    unit_shapes = (
        ((2, hidden, width), 1, first_order),
        ((2, width, hidden), 0, second_order),
        ((2, width, hidden), 0, first_order),
        ((2, local, width), 0, second_order),
        ((2, width, local), 0, first_order),
        ((2, width, local), 0, second_order),
        ((2, width, local), 0, second_order),
        ((2, width, local), 0, second_order),
    )
    received = []
    for full, axis, _ in unit_shapes:
        def cut(parts, full=full, axis=axis):
            return tuple(n // parts if d == 1 + axis else n for d, n in enumerate(full))

        received += [vmem(cut(2 << k)) for k in range(PIECE_BITS)]
        received += [vmem(cut(1 << PIECE_BITS))] * extras
        received += [vmem(cut(1 << PIECE_BITS)[1:])] * 2
    stages = len(unit_shapes) * (2 * PIECE_BITS + extras + 1) + bits + 2 + 8
    results = pl.pallas_call(
        functools.partial(backward_kernel, dp_size, extras, unit_shapes),
        out_shape=[shape(full[1:], BF) for full, _, _ in unit_shapes]
        + [shape((own, width), BF), shape((8, width), F32)],
        in_specs=[ANY] * 26 + [INNER] * 3,
        out_specs=[ANY] * (len(unit_shapes) + 2),
        scratch_shapes=[vmem(full) for full, _, _ in unit_shapes]
        + received
        + [
            vmem((width, tokens)), vmem((2, local, tokens)), vmem((2, hidden, tokens)),
            vmem((2, tokens, hidden)), vmem((2, tokens, hidden)), vmem((tokens, width)), vmem(heads), vmem(heads),
            vmem(heads), vmem(heads), vmem(heads), vmem(heads, F32), vmem(heads, F32), vmem(heads, F32),
            vmem((2, local, local // 2)), vmem((2, 4, width, local)), vmem((2, local, width)), vmem((own, width), F32),
            vmem((bits + 3, 8, width), F32), vmem((bits + 2, 8, width), F32), vmem((own, width)),
            vmem((tokens, width)), vmem(heads), vmem((2, 4, tokens, local)), vmem((tokens, tokens)),
            vmem((tokens, tokens)), vmem((tokens, local), F32), vmem((tokens, local), F32),
            vmem((tokens, local), F32), vmem((2, local, local // 2)), vmem((2, local, local // 2)),
            vmem((own, width)), vmem((own, width)), vmem((own, width), F32), vmem((own, width)),
            pltpu.SemaphoreType.DMA((stages,)), pltpu.SemaphoreType.DMA((stages,)), pltpu.SemaphoreType.DMA((48,)),
        ],
        compiler_params=pltpu.CompilerParams(collective_id=1, has_side_effects=True, vmem_limit_bytes=63 << 20),
    )(
        *kept, query_weight, key_weight, value_weight, gate_weight, joined, out_weight, ow, dres, gain, inputs,
        segr, segc, gain_one,
    )
    down, left, right, out, query, key, value, gate, block_grad, gains = results
    wide = [a.astype(F32) for a in (query, key, value, gate, out, left, right, down)]
    return (block, block_grad, *wide, gains[1], gains[0])


def solution(mesh):
    row, column = P("tensor", None), P(None, "tensor")
    tokens = P(("dp", "tensor"), None)
    return jax.shard_map(
        functools.partial(per_device, mesh.shape["dp"]),
        mesh=mesh,
        in_specs=(
            tokens, P("dp", None), column, column, column, column, row, column, column, row, P(), P(), tokens,
        ),
        out_specs=(tokens, tokens, column, column, column, column, row, column, column, row, P(), P()),
        check_vma=False,
    )
```

time: 722 us -> 288 us (0.40)
  waiting for transfers between devices: 539 us -> 0 us
  Pallas kernels: 0 us -> 265 us
  matrix products: 74 us -> 0 us
  blocking collectives: 42.2 us -> 0 us
  between operations: 14.9 us -> 0.68 us
  local copies, waits for them, and re-layouts: 24 us -> 12.9 us
  other arithmetic: 18.6 us -> 8.31 us
    pallas_call x0 -> x2, Pallas kernels: none -> 265 us  [the longest x1 138 us: per_device(): pl.pallas_call(functools.partial(backward_kernel, dp_size, extras, unit_s...]
    psum x1 -> x0, waiting for transfers between devices: 191 us -> none  [per_device(): lax.psum((query_grad, key_grad, value_grad, gate_grad, out_grad, left_gra...]
    all_gather x4 -> x0, waiting for transfers between devices: 175 us -> none  [the longest x1 46.4 us: per_device(): lax.all_gather(resid_grad.astype(jnp.bfloat16), 'tensor', axis=0, tiled=T...]
    reduce_scatter x4 -> x0, waiting for transfers between devices: 172 us -> none  [the longest x1 75.6 us: per_device(): lax.psum_scatter(jnp.dot(gated, out_weight, preferred_element_type=jnp.fl...]
    dot_general x21 -> x0, matrix products: 74 us -> none  [the longest x1 6.34 us: per_device(): jnp.einsum('td,fd->tf', down_in, down_weight, preferred_element_type=jnp....]
    psum x1 -> x0, blocking collectives: 42.2 us -> none  [per_device(): lax.psum((first_part, second_part), ('dp', 'tensor'))]
    unnamed x127 -> x26, local copies, waits for them, and re-layouts: 21.8 us -> 9.75 us
    reduce_sum x5 -> x0, other arithmetic: 7.36 us -> none  [the longest x2 2.95 us: rms_scale(): return lax.rsqrt(jnp.mean(values * values, axis=-1, keepdims=True) + EPS)]
  transfers between devices with their start and end apart: 9 -> 0, of which waited for: 9 -> 0; matrix products, arithmetic and copies ran while one was open for 5% -> 0% of each run, Pallas kernels for 0% -> 0%
where the time goes in v2:
time: 288 us; the launch traced here: 287 us
  Pallas kernels  265 us (92%)
  local copies, waits for them, and re-layouts  12.9 us (4%)
  other arithmetic  8.31 us (3%)
    pallas_call x1, Pallas kernels, per_device(): pl.pallas_call(functools.partial(backward_kernel, dp_size, extras, unit_s...  138 us
    pallas_call x1, Pallas kernels, per_device(): pl.pallas_call(functools.partial(forward_kernel, dp_size), out_shape=save...  127 us
    unnamed x26, local copies, waits for them, and re-layouts  9.75 us
    convert_element_type x6, other arithmetic, per_device(): a.astype(F32)  8.31 us

profile of v2, /device:TPU:0, one launch (start us, length us, event | category | flops | bytes accessed | tf_op | source)
XLA Modules:
  0.0 286.9 jit_solution(5609733069446358207)
XLA Ops:
  0.6 1.7 copy.29.segc_ref
  2.4 2.7 copy.30.wl
  5.0 0.0 copy-done.2
  5.0 1.6 copy.31.wr
  6.6 127.2 %shard_map.220 = (bf16[1024,512]{1,0:T(8,128)(2,1)}, bf16[1024,512]{1,0:T(8,128)(2,1)}, bf16[2,256,512]{2,1,0:T(8,128)(2,1)}, bf16[2,704,512]{2,1,0:T(8,128)(2,1...) custom-call(bf16[256,1024]{1,0:T(8,128)(2,1)} %x_hbm.3, ...), custom_call_target="tpu_custom_call" | custom-call | tf_op jit(solution)/shard_map/pallas_call | solution.py:780
  133.8 137.8 %shard_map.221 = (bf16[704,1024]{1,0:T(8,128)(2,1)}, bf16[1024,704]{1,0:T(8,128)(2,1)}, bf16[1024,704]{1,0:T(8,128)(2,1)}, bf16[256,1024]{1,0:T(8,128)(2,1)}, bf...) custom-call(bf16[1024,512]{1,0:T(8,128)(2,1)} %get-tuple-element.44., ...), custom_call_target="tpu_custom_call" | custom-call | tf_op jit(solution)/shard_map/pallas_call | solution.py:829
  271.6 0.0 copy-start.7
  271.6 1.4 fusion
  273.0 2.1 convert_element_type.24
  275.2 0.0 copy-done.7
  275.2 1.0 convert_element_type.25
  276.2 0.0 copy-done.6
  276.2 1.0 convert_element_type.26
  277.3 0.0 copy-done.5
  277.3 1.0 convert_element_type.27
  278.3 0.0 copy-done.4
  278.3 1.1 convert_element_type.28
  279.4 0.0 copy-done.1
  279.4 2.0 copy.33
  281.4 0.0 copy-done
  281.4 2.0 copy.34
  283.3 1.9 convert_element_type.31
  285.3 0.8 copy.37
  286.1 0.8 copy.38
  (12 shorter events, 0.0 us)
Async XLA Ops:
  2.4 2.7 copy-start.2
  271.6 3.6 %copy-start.7 = (bf16[1024,256]{1,0:T(8,128)(2,1)S(1)}, bf16[1024,256]{1,0:T(8,128)(2,1)}, u32[]{:S(2)}) copy-start(bf16[1024,256]{1,0:T(8,128)(2,1)} %get-tuple-element.66) | copy-start | bytes 1572868
  273.0 3.2 %copy-start.6 = (bf16[1024,256]{1,0:T(8,128)(2,1)S(1)}, bf16[1024,256]{1,0:T(8,128)(2,1)}, u32[]{:S(2)}) copy-start(bf16[1024,256]{1,0:T(8,128)(2,1)} %get-tuple-element.67) | copy-start | bytes 1572868
  275.2 2.1 copy-start.5
  276.2 2.1 copy-start.4
  277.3 2.1 copy-start.1
  279.4 2.0 copy-start
  281.4 2.0 copy-start.3
  283.3 1.9 copy-start.8
  283.3 2.7 copy-start.9

commit v3 on v2

v3 whole, which is shorter than its diff:
```python
import functools
import itertools

import jax
import jax.numpy as jnp
from jax import lax
from jax.experimental import pallas as pl
from jax.experimental.pallas import tpu as pltpu
from jax.sharding import PartitionSpec as P

EPS = 1e-05
HEAD = 64
BF = jnp.bfloat16
F32 = jnp.float32
MESH = pl.DeviceIdType.MESH
ANY = pl.BlockSpec(memory_space=pl.ANY)
INNER = pl.BlockSpec(memory_space=pltpu.VMEM)
PIECE_BITS = 3


def dot(a, b):
    return lax.dot_general(a, b, (((1,), (0,)), ((), ())), preferred_element_type=F32)


def dot_t(a, b):
    return lax.dot_general(a, b, (((1,), (1,)), ((), ())), preferred_element_type=F32)


class Place:
    def __init__(self, dp_size):
        self.i = lax.axis_index("dp")
        self.t = lax.axis_index("tensor")
        self.half = lax.rem(self.t, 2)
        self.pair = self.t // 2
        self.bits = dp_size.bit_length() - 1
        self.mate = {"tensor": self.t + 1 - 2 * self.half}
        self.twin = {"tensor": self.t + 2 - 4 * self.pair}

    def bit(self, b):
        return lax.rem(self.i // (1 << b), 2)

    def over(self, b):
        return {"dp": self.i + (1 << b) * (1 - 2 * self.bit(b))}

    def greet(self):
        barrier = pltpu.get_barrier_semaphore()
        peers = [self.mate, self.twin] + [self.over(b) for b in range(self.bits)]
        for peer in peers:
            pl.semaphore_signal(barrier, inc=1, device_id=peer, device_id_type=MESH)

        def all_here():
            pl.semaphore_wait(barrier, len(peers))

        return all_here


class Links:
    def __init__(self, send_sem, recv_sem):
        self.send_sem, self.recv_sem, self.count, self.open = send_sem, recv_sem, 0, []

    def start(self, source, target, peer):
        copy = pltpu.make_async_remote_copy(
            src_ref=source,
            dst_ref=target,
            send_sem=self.send_sem.at[self.count],
            recv_sem=self.recv_sem.at[self.count],
            device_id=peer,
            device_id_type=MESH,
        )
        self.count += 1
        copy.start()
        self.open.append(copy)
        return copy

    def settle(self, *copies):
        for copy in copies:
            copy.wait_send()
        self.open = [other for other in self.open if all(other is not copy for copy in copies)]

    def finish(self):
        self.settle(*self.open)


class Moves:
    def __init__(self, sem):
        self.sem, self.count, self.open = sem, 0, []

    def start(self, source, target):
        copy = pltpu.make_async_copy(source, target, self.sem.at[self.count])
        self.count += 1
        copy.start()
        self.open.append(copy)
        return copy

    def wait(self, copy):
        copy.wait()
        self.open = [other for other in self.open if other is not copy]

    def finish(self):
        for copy in list(self.open):
            self.wait(copy)


def part(ref, lead, axis, first, count):
    window = pl.ds(first, count)
    return ref.at[lead + ((window, slice(None)) if axis == 0 else (slice(None), window))]


def piece_of(place, order):
    total = 0
    for b in order:
        total = 2 * total + place.bit(b)
    return total


class Gather:
    def __init__(self, place, links, ref, lead, axis, order):
        self.place, self.links, self.ref, self.lead, self.axis, self.order = place, links, ref, lead, axis, order
        self.size = ref.shape[len(ref.shape) - 2 + axis] // (1 << len(order))
        self.piece = piece_of(place, order)
        self.copy, self.stage, self.sent = None, 0, []

    def block(self, shard, width):
        first = (self.piece // width) * (width * self.size)
        return part(self.ref, (shard,) + self.lead, self.axis, pl.multiple_of(first, self.size), width * self.size)

    def begin(self):
        self.copy = self.links.start(self.block(0, 1), self.block(1, 1), self.place.twin)
        self.sent.append(self.copy)

    def advance(self):
        self.copy.wait_recv()
        if self.stage < len(self.order):
            block = self.block(1, 1 << self.stage)
            self.copy = self.links.start(block, block, self.place.over(self.order[-1 - self.stage]))
            self.sent.append(self.copy)
        self.stage += 1


def rows_loop(count, size, body):
    def step(k, carry):
        body(pl.multiple_of(k * size, size))
        return carry

    lax.fori_loop(0, count // size, step, 0)


def softplus_and_slope(values):
    tail = jnp.exp(-jnp.abs(values))
    soft = jnp.maximum(values, 0.0) + jnp.log1p(tail)
    slope = jnp.where(values >= 0, 1.0, tail) / (1.0 + tail)
    return soft, slope


def sigmoid(values):
    tail = jnp.exp(-jnp.abs(values))
    return jnp.where(values >= 0, 1.0, tail) / (1.0 + tail)


def head_of(shape, axis):
    return lax.broadcasted_iota(jnp.int32, shape, axis) // HEAD


def same_head(width):
    return head_of((width, width), 0) == head_of((width, width), 1)


def head_mean(values):
    ones = jnp.where(same_head(values.shape[-1]), 1.0 / HEAD, 0.0).astype(BF)
    return dot(values.astype(BF), ones)


def fold(state):
    width = state.shape[-1]
    state = jnp.where(same_head(width), state, 0.0)
    return (state[:, : width // 2] + state[:, width // 2 :]).astype(BF)


def unfold(state):
    both = jnp.concatenate((state, state), axis=1)
    return jnp.where(same_head(both.shape[-1]), both, jnp.zeros_like(both))


def only_head(values, head):
    return jnp.where(head_of(values.shape, 1) == head, values, jnp.zeros_like(values))


class Reduce:
    def __init__(self, place, links, moves, grad, axis, order, halves, credits, twin_recv, out):
        self.place, self.links, self.moves = place, links, moves
        self.grad, self.axis, self.order = grad, axis, order
        self.halves, self.twin_recv, self.out = halves, twin_recv, out
        self.extra = credits
        self.size = grad.shape[1 + axis] // (1 << len(order))
        self.piece = piece_of(place, order)
        self.stage, self.copy, self.local = 0, None, None
        self.steps = len(order) + len(self.extra) + 1 + len(order)

    def first_of(self, width):
        return pl.multiple_of((self.piece // width) * (width * self.size), self.size)

    def grad_part(self, lead, first, width):
        return part(self.grad, lead, self.axis, pl.multiple_of(first, self.size), width * self.size)

    def out_part(self, width):
        return part(self.out, (), self.axis, self.first_of(width), width * self.size)

    def begin(self):
        shards, folds = (slice(None),), len(self.order)
        k = self.stage
        if k < folds:
            width = 1 << (folds - 1 - k)
            bit = self.place.bit(self.order[k])
            away = self.first_of(width) + (1 - 2 * bit) * (width * self.size)
            self.copy = self.links.start(
                self.grad_part(shards, away, width), self.halves[k], self.place.over(self.order[k])
            )
            return
        k -= folds
        if k < len(self.extra):
            peer = self.place.over(folds + k)
            pl.semaphore_signal(self.extra[k], inc=1, device_id=peer, device_id_type=MESH)
            pl.semaphore_wait(self.extra[k], 1)
            source = self.grad_part(shards, self.first_of(1), 1)
            self.copy = self.links.start(source, self.halves[-1], peer)
            return
        k -= len(self.extra)
        if k == 0:
            source = self.grad_part((1,), self.first_of(1), 1)
            self.copy = self.links.start(source, self.twin_recv, self.place.twin)
            return
        k -= 1
        block = self.out_part(1 << k)
        source = self.grad_part((0,), self.first_of(1), 1) if k == 0 else block
        self.copy = self.links.start(source, block, self.place.over(self.order[folds - 1 - k]))
        if k == 0:
            self.local = self.moves.start(source, block)

    def add(self, recv, width):
        rows, chunk = recv.shape[-2], 32
        first = self.first_of(width)

        def body(at):
            for shard in range(recv.shape[0] if len(recv.shape) == 3 else 1):
                if self.axis == 0:
                    where = (shard, pl.ds(pl.multiple_of(first + at, chunk), chunk), slice(None))
                else:
                    where = (shard, pl.ds(at, chunk), pl.ds(first, width * self.size))
                came = recv[(shard,) * (len(recv.shape) - 2) + (pl.ds(at, chunk), slice(None))]
                self.grad[where] = self.grad[where] + came

        rows_loop(rows, chunk, body)

    def advance(self):
        if self.stage >= self.steps:
            return
        folds = len(self.order)
        self.copy.wait_recv()
        k = self.stage
        if k < folds:
            self.add(self.halves[k], 1 << (folds - 1 - k))
        elif k < folds + len(self.extra):
            self.links.settle(self.copy)
            self.add(self.halves[-1], 1)
        elif k == folds + len(self.extra):
            self.add(self.twin_recv, 1)
        elif self.local is not None:
            self.moves.wait(self.local)
            self.local = None
        self.stage += 1
        if self.stage < self.steps:
            self.begin()

    def over(self):
        return self.stage >= self.steps


def marks_of(place, segr_ref, segc, tokens):
    offset = pl.multiple_of(place.pair * tokens, tokens)
    across = segr_ref[:, pl.ds(offset, tokens)].astype(F32)
    segc[...] = jnp.broadcast_to(across, (8, tokens)).T[:, :1]
    return across, segr_ref[:, tokens - 1 : tokens].astype(F32)


def doc_mask(across, segc, mask_ref, tokens, later):
    def body(first):
        at = first + lax.broadcasted_iota(jnp.int32, (64, tokens), 0)
        col = lax.broadcasted_iota(jnp.int32, (64, tokens), 1)
        order = col >= at if later else col <= at
        same = segc[pl.ds(first, 64), :] == across
        mask_ref[pl.ds(first, 64), :] = jnp.where(same & order, 1.0, 0.0).astype(BF)

    rows_loop(tokens, 64, body)


def layer_kernel(
    dp_size, extras, hidden, pad,
    x_hbm, segr_ref, wq, wk, wv, wz, wo, wl, wr, wd, g1_ref, g2_ref, cot_hbm,
    down_out, left_out, right_out, ow_out, query_out, key_out, value_out, gate_out, block_out, grad_out, gains_out,
    x_ref, segc, normed, normed_t, joined, ow, lrw, dw, qp, kp, vl, sq, sk, hn, rr, sz, gated, mask, mask_t,
    state_send, state_recv, meet_send, meet_recv, trade_send, trade_recv, back_send, back_recv,
    resid, own_sum, second, cot, hid, dres, dm, djoined, dq, dk, dv, gains, gains_recv,
    grad_d, grad_l, grad_r, grad_o,
    *rest,
):
    *received, send_sem, recv_sem, move_sem, free_sem, credit_sem = rest
    received, tickets = list(received), itertools.count()
    place = Place(dp_size)
    links, moves = Links(send_sem, recv_sem), Moves(move_sem)
    own, width = x_ref.shape
    tokens = 2 * own
    local = qp.shape[-1]
    mine = pl.multiple_of(place.half * own, own)
    theirs = pl.multiple_of((1 - place.half) * own, own)
    lw, rw = lrw.at[:, :hidden, :], lrw.at[:, hidden:, :]
    product, dleft, dright = (slice(n * pad, n * pad + hidden) for n in range(3))
    dres_all = normed

    all_here = place.greet()
    x_in = moves.start(x_hbm, x_ref)
    joined_in = [moves.start(w, joined.at[0, j]) for j, w in enumerate((wq, wk, wv, wz))]
    ow_in = moves.start(wo, ow.at[0])
    ffn_in = [moves.start(w, v.at[0]) for w, v in ((wl, lw), (wr, rw), (wd, dw))]
    cot_in = moves.start(cot_hbm, cot.at[pl.ds(mine, own), :])
    moves.wait(x_in)

    def first_norm(first):
        values = x_ref[pl.ds(first, 32), :].astype(F32)
        scale = lax.rsqrt(jnp.mean(values * values, axis=-1, keepdims=True) + EPS)
        normed[pl.ds(mine + first, 32), :] = (values * scale * g1_ref[...]).astype(BF)

    rows_loop(own, 32, first_norm)
    for copy in joined_in:
        moves.wait(copy)
    all_here()
    block = normed.at[pl.ds(mine, own), :]
    normed_copy = links.start(block, block, place.mate)
    first_order, second_order = (0, 1, 2), (0, 2, 1)
    join_a = Gather(place, links, joined, (pl.ds(0, 2),), 0, first_order)
    join_b = Gather(place, links, joined, (pl.ds(2, 2),), 0, second_order)
    gather_o = Gather(place, links, ow, (), 1, second_order)
    gather_l = Gather(place, links, lw, (), 1, first_order)
    gather_r = Gather(place, links, rw, (), 1, second_order)
    gather_d = Gather(place, links, dw, (), 1, first_order)
    join_a.begin()
    join_b.begin()
    moves.wait(ow_in)
    gather_o.begin()

    def advance(*units):
        for unit in units:
            unit.advance()

    def project(shard, first, which):
        rows = normed[pl.ds(first, own), :]
        at = pl.ds(first, own)
        for j in which:
            raw = dot(rows, joined[shard, j])
            if j == 2:
                vl[shard, at, :] = raw.astype(BF)
            elif j == 3:
                sz[shard, at, :] = sigmoid(raw).astype(BF)
            else:
                soft, slope = softplus_and_slope(raw)
                (qp, kp)[j][shard, at, :] = soft.astype(BF)
                (sq, sk)[j][shard, at, :] = slope.astype(BF)

    project(0, mine, (1, 2, 0, 3))
    for copy in ffn_in:
        moves.wait(copy)
    gather_l.begin()
    gather_r.begin()
    gather_d.begin()
    across, last = marks_of(place, segr_ref, segc, tokens)
    doc_mask(across, segc, mask, tokens, False)
    moves.wait(cot_in)
    normed_copy.wait_recv()
    cot_block = cot.at[pl.ds(mine, own), :]
    cot_copy = links.start(cot_block, cot_block, place.mate)
    project(0, theirs, (1, 2))
    near = segc[...] == last
    state_copy = [None, None]

    def send_state(shard):
        keys = jnp.where(near, kp[shard].astype(F32), 0.0).astype(BF)
        state_send[shard] = fold(dot(keys.T, vl[shard]))
        state_copy[shard] = links.start(state_send.at[shard], state_recv.at[1 - shard], place.twin)

    send_state(0)
    project(0, theirs, (0, 3))
    advance(join_a, join_b, gather_o)

    def mix(shard):
        def one(head, carry):
            for r in range(2):
                seen = (r + 1) * own
                at = slice(r * own, (r + 1) * own)
                raw = dot_t(only_head(qp[shard, at, :], head), kp[shard, :seen, :])
                scores = raw.astype(BF) * mask[at, :seen]
                dq[at, :] += dot(scores, only_head(vl[shard, :seen, :], head))
            return carry

        dq[...] = jnp.zeros(dq.shape, F32)
        lax.fori_loop(0, local // HEAD, one, 0)

    first_half, second_half = place.pair == 0, place.pair == 1

    def open_gate(shard):
        state_copy[1 - shard].wait_recv()
        query = jnp.where(near & second_half, qp[shard].astype(F32), 0.0).astype(BF)
        mixed = dq[...] + dot(query, unfold(state_recv[shard]))
        scale = lax.rsqrt(head_mean(mixed * mixed) + EPS)
        norm = mixed * scale
        rr[shard] = scale.astype(BF)
        hn[shard] = norm.astype(BF)
        gated[shard] = (norm * sz[shard].astype(F32)).astype(BF)

    mix(0)
    advance(join_a, join_b, gather_o, gather_l)
    advance(join_a, join_b, gather_o, gather_r, gather_l)
    advance(join_a, join_b, gather_o)
    for first in (mine, theirs):
        project(1, first, (1, 2))
    send_state(1)
    open_gate(0)
    advance(gather_d, gather_r, gather_l)
    for first in (mine, theirs):
        project(1, first, (0, 3))
    advance(gather_d, gather_r, gather_l)
    mix(1)
    advance(gather_d, gather_r)
    open_gate(1)

    def branch(first):
        at = pl.ds(first, own)
        return dot(gated[0, at, :], ow[0]) + dot(gated[1, at, :], ow[1])

    trade_send[...] = branch(theirs).astype(BF)
    branch_copy = links.start(trade_send, trade_recv, place.mate)
    own_sum[...] = branch(mine)
    advance(gather_d)
    for c in range(0, width, 256):
        normed_t[c : c + 256, :] = normed[:, c : c + 256].T
    doc_mask(across, segc, mask_t, tokens, True)
    branch_copy.wait_recv()

    def second_norm(first):
        at = pl.ds(first, 32)
        values = x_ref[at, :].astype(F32) + own_sum[at, :] + trade_recv[at, :].astype(F32)
        resid[at, :] = values
        scale = lax.rsqrt(jnp.mean(values * values, axis=-1, keepdims=True) + EPS)
        second[pl.ds(mine + first, 32), :] = (values * scale * g2_ref[...]).astype(BF)

    rows_loop(own, 32, second_norm)
    block = second.at[pl.ds(mine, own), :]
    second_copy = links.start(block, block, place.mate)
    cot_copy.wait_recv()

    def hidden_grad(first):
        at = pl.ds(first, own)

        def one(shard, carry):
            hid[shard, at, dleft] = dot_t(cot[at, :], dw[shard]).astype(BF)
            return carry

        lax.fori_loop(0, 2, one, 0)

    def unit_rows(first):
        at = pl.ds(first, own)

        def one(shard, carry):
            left = dot_t(second[at, :], lw[shard])
            right = dot_t(second[at, :], rw[shard])
            grad = hid[shard, at, dleft].astype(F32)
            hid[shard, at, product] = (left * right).astype(BF)
            hid[shard, at, dleft] = (grad * right).astype(BF)
            hid[shard, at, dright] = (grad * left).astype(BF)
            return carry

        lax.fori_loop(0, 2, one, 0)

    hidden_grad(mine)
    unit_rows(mine)
    hidden_grad(theirs)
    second_copy.wait_recv()
    unit_rows(theirs)

    def back(first):
        at = pl.ds(first, own)
        return (
            dot(hid[0, at, dleft], lw[0])
            + dot(hid[0, at, dright], rw[0])
            + dot(hid[1, at, dleft], lw[1])
            + dot(hid[1, at, dright], rw[1])
        )

    def ffn(first):
        at = pl.ds(first, own)
        return dot(hid[0, at, product], dw[0]) + dot(hid[1, at, product], dw[1])

    back_send[...] = back(theirs).astype(BF)
    back_copy = links.start(back_send, back_recv, place.mate)
    own_sum[...] = back(mine)

    def make_unit(grad, axis, order, out, first_half_ref=None):
        folds = len(order)
        halves = [received.pop(0) for _ in range(folds - (first_half_ref is not None))]
        if first_half_ref is not None:
            halves = [first_half_ref] + halves
        credits = [credit_sem.at[next(tickets)] for _ in range(extras)]
        return Reduce(place, links, moves, grad, axis, order, halves, credits, received.pop(0), out)

    def split_units(grad, out):
        rows = grad.shape[1] // 2
        return [
            make_unit(grad.at[:, n * rows : (n + 1) * rows, :], 1, order, out.at[n * rows : (n + 1) * rows, :])
            for n, order in enumerate((first_order, second_order))
        ]

    down_units, left_units, right_units = (
        split_units(g, o) for g, o in ((grad_d, down_out), (grad_l, left_out), (grad_r, right_out))
    )
    ow_units = split_units(grad_o, ow_out)
    joined_units = [
        make_unit(
            lrw.at[:, :width, j * local : (j + 1) * local], 0, order, out,
            hid.at[:, : width // 2, j * local : (j + 1) * local],
        )
        for j, (order, out) in enumerate(
            zip(
                (first_order, second_order, first_order, second_order),
                (query_out, key_out, value_out, gate_out),
            )
        )
    ]
    live = []

    def launch(*units):
        for unit in units:
            unit.begin()
            live.append(unit)

    def step_all():
        for unit in live:
            unit.advance()

    def hidden_outer(units, grad, left, right):
        def one(shard, carry):
            for c in range(0, hidden, 256):
                high = min(c + 256, hidden)
                grad[shard, c:high, :] = dot(hid[shard, :, left.start + c : left.start + high].T, right[...]).astype(BF)
            return carry

        lax.fori_loop(0, 2, one, 0)
        launch(*units)

    hidden_outer(down_units, grad_d, product, cot)
    hidden_outer(left_units, grad_l, dleft, second)
    advance(*down_units)
    back_copy.wait_recv()

    gains[0] = jnp.zeros(gains.shape[1:], F32)

    def residual_back(first):
        at = pl.ds(first, 32)
        values = resid[at, :]
        scale = lax.rsqrt(jnp.mean(values * values, axis=-1, keepdims=True) + EPS)
        grad = own_sum[at, :] + back_recv[at, :].astype(F32)
        gains[0, 0:1, :] += jnp.sum(grad * values * scale, axis=0, keepdims=True)
        weighted = grad * g2_ref[...]
        inner = jnp.mean(weighted * values, axis=-1, keepdims=True)
        upstream = cot[pl.ds(mine + first, 32), :].astype(F32)
        total = upstream + scale * weighted - values * (scale * scale * scale * inner)
        dres[at, :] = total
        dres_all[pl.ds(mine + first, 32), :] = total.astype(BF)

    links.settle(normed_copy)
    rows_loop(own, 32, residual_back)
    block = dres_all.at[pl.ds(mine, own), :]
    dres_copy = links.start(block, block, place.mate)
    hidden_outer(right_units, grad_r, dright, second)
    advance(*left_units)
    links.settle(back_copy)
    back_send[...] = ffn(theirs).astype(BF)

    def add_ffn(first):
        resid[...] += ffn(first)

    add_ffn(mine)
    advance(*right_units)
    pl.semaphore_signal(free_sem, inc=1, device_id=place.over(0), device_id_type=MESH)
    advance(*down_units)
    dres_copy.wait_recv()
    ffn_copy = links.start(back_send, back_recv, place.mate)

    def gate_back(shard, carry):
        grad = dot_t(dres_all[...], ow[shard])
        opened, norm = sz[shard].astype(F32), hn[shard].astype(F32)
        djoined[shard, 3] = (grad * norm * opened * (1.0 - opened)).astype(BF)
        inner = grad * opened
        dm[shard] = (rr[shard].astype(F32) * (inner - norm * head_mean(inner * norm))).astype(BF)
        return carry

    lax.fori_loop(0, 2, gate_back, 0)
    meets = []
    for shard in range(2):
        query = jnp.where(near, qp[shard].astype(F32), 0.0).astype(BF)
        meet_send[shard] = fold(dot(query.T, dm[shard]))
        meets.append(links.start(meet_send.at[shard], meet_recv.at[1 - shard], place.twin))

    def out_outer(shard, carry):
        grad_o[shard] = dot(gated[shard].T, dres_all[...]).astype(BF)
        return carry

    lax.fori_loop(0, 2, out_outer, 0)
    launch(*ow_units)
    gathers = (join_a, join_b, gather_o, gather_l, gather_r, gather_d)
    for unit in gathers:
        links.settle(*unit.sent)
    pl.semaphore_wait(free_sem, 1)

    def project_back(j):
        def body(first):
            def one(shard, carry):
                part_grad = dot(normed_t[pl.ds(first, 256), :], djoined[shard, j])
                lrw[shard, pl.ds(first, 256), j * local : (j + 1) * local] = part_grad.astype(BF)
                return carry

            lax.fori_loop(0, 2, one, 0)

        rows_loop(width, 256, body)
        launch(joined_units[j])

    project_back(3)
    step_all()

    def mix_back(shard):
        dq[...] = jnp.where(near & second_half, dot_t(dm[shard], unfold(state_recv[shard])), 0.0)
        dk[...] = jnp.zeros(dk.shape, F32)
        dv[...] = jnp.zeros(dv.shape, F32)

        def one(head, carry):
            for r in range(2):
                seen = (r + 1) * own
                at = slice(r * own, (r + 1) * own)
                grad_r, query_r = dm[shard, at, :], qp[shard, at, :]
                grad_h, query_h = only_head(grad_r, head), only_head(query_r, head)
                keys_h = only_head(kp[shard, :seen, :], head)
                vals_h = only_head(vl[shard, :seen, :], head)
                ds = dot_t(grad_r, vals_h).astype(BF) * mask[at, :seen]
                dq[at, :] += dot(ds, keys_h)
                st = dot_t(keys_h, query_r).astype(BF) * mask_t[:seen, at]
                dv[:seen, :] += dot(st, grad_h)
                dst = dot_t(vals_h, grad_r).astype(BF) * mask_t[:seen, at]
                dk[:seen, :] += dot(dst, query_h)
            return carry

        lax.fori_loop(0, local // HEAD, one, 0)

    for shard in range(2):
        mix_back(shard)
        if shard == 0:
            step_all()
        meets[1 - shard].wait_recv()
        meet = unfold(meet_recv[shard])
        marks = near & first_half
        djoined[shard, 2] = (dv[...] + jnp.where(marks, dot(kp[shard], meet), 0.0)).astype(BF)
        from_meet = jnp.where(marks, dot_t(vl[shard], meet), 0.0)
        djoined[shard, 1] = ((dk[...] + from_meet) * sk[shard].astype(F32)).astype(BF)
        djoined[shard, 0] = (dq[...] * sq[shard].astype(F32)).astype(BF)

    project_back(0)
    project_back(1)
    project_back(2)
    step_all()

    def normed_back(first):
        at = pl.ds(first, own)
        own_sum[...] = jnp.zeros(own_sum.shape, F32)

        def one(k, carry):
            own_sum[...] += dot_t(djoined[k // 4, lax.rem(k, 4), at, :], joined[k // 4, lax.rem(k, 4)])
            return carry

        lax.fori_loop(0, 8, one, 0)

    links.settle(branch_copy)
    normed_back(theirs)
    trade_send[...] = own_sum[...].astype(BF)
    trade_copy = links.start(trade_send, trade_recv, place.mate)
    step_all()
    normed_back(mine)
    ffn_copy.wait_recv()
    links.settle(ffn_copy)

    def finish_out(first):
        at = pl.ds(first, 32)
        back_send[at, :] = (resid[at, :] + back_recv[at, :].astype(F32)).astype(BF)

    rows_loop(own, 32, finish_out)
    moves.start(back_send, block_out)
    step_all()
    trade_copy.wait_recv()
    links.settle(trade_copy)

    def finish_grad(first):
        at = pl.ds(first, 32)
        values = x_ref[at, :].astype(F32)
        scale = lax.rsqrt(jnp.mean(values * values, axis=-1, keepdims=True) + EPS)
        grad = own_sum[at, :] + trade_recv[at, :].astype(F32)
        gains[0, 1:2, :] += jnp.sum(grad * values * scale, axis=0, keepdims=True)
        weighted = grad * g1_ref[...]
        inner = jnp.mean(weighted * values, axis=-1, keepdims=True)
        trade_send[at, :] = (dres[at, :] + scale * weighted - values * (scale * scale * scale * inner)).astype(BF)

    rows_loop(own, 32, finish_grad)
    moves.start(trade_send, grad_out)

    peers = [place.over(b) for b in range(place.bits)] + [place.mate, place.twin]
    for n, peer in enumerate(peers):
        copy = links.start(gains.at[n], gains_recv.at[n], peer)
        step_all()
        copy.wait_recv()
        gains[n + 1] = gains[n] + gains_recv[n]
    moves.start(gains.at[len(peers)], gains_out)
    while not all(unit.over() for unit in live):
        step_all()
    moves.finish()
    links.finish()


def widen_kernel(count, passed, *refs):
    sources, refs = refs[: count + passed], refs[count + passed :]
    targets, refs = refs[: count + passed], refs[count + passed :]
    narrow, wide, (in_sem, out_sem) = refs[:count], refs[count : 2 * count], refs[2 * count :]
    loads = [pltpu.make_async_copy(sources[n], narrow[n], in_sem.at[n]) for n in range(count)]
    stores = [pltpu.make_async_copy(wide[n], targets[n], out_sem.at[n]) for n in range(count)]
    stores += [
        pltpu.make_async_copy(sources[n], targets[n], out_sem.at[n]) for n in range(count, count + passed)
    ]
    for copy in loads + stores[count:]:
        copy.start()
    for n in range(count):
        loads[n].wait()

        def body(first, n=n):
            wide[n][pl.ds(first, 64), :] = narrow[n][pl.ds(first, 64), :].astype(F32)

        rows_loop(narrow[n].shape[0], 64, body)
        stores[n].start()
    for copy in stores:
        copy.wait()


def vmem(shape, dtype=BF):
    return pltpu.VMEM(shape, dtype)


def per_device(
    dp_size,
    inputs, segments, query_weight, key_weight, value_weight, gate_weight, out_weight, left_weight, right_weight,
    down_weight, norm_first, norm_second, cotangent,
):
    own, width = inputs.shape
    tokens = 2 * own
    local = query_weight.shape[1]
    hidden = left_weight.shape[1]
    pad = -(-hidden // 128) * 128
    bits = dp_size.bit_length() - 1
    extras = bits - PIECE_BITS
    shape = jax.ShapeDtypeStruct
    heads, state = (2, tokens, local), (2, local, local // 2)
    grads = [(hidden, width)] * 3 + [(local, width)] + [(width, local)] * 4

    def buffers(rows, columns, axis, first):
        def cut(parts):
            return (2, rows // parts, columns) if axis == 0 else (2, rows, columns // parts)

        eighth = cut(1 << PIECE_BITS)
        kept = [vmem(cut(2 << k)) for k in range(first, PIECE_BITS)]
        return kept + [vmem(eighth[1:])]

    received = []
    for rows in (hidden // 2,) * 6 + (local // 2,) * 2:
        received += buffers(rows, width, 1, 0)
    for _ in range(4):
        received += buffers(width, local, 0, 1)
    copies = 12 * (2 * PIECE_BITS + extras + 1) + 6 * (PIECE_BITS + 1) + bits + 16
    results = pl.pallas_call(
        functools.partial(layer_kernel, dp_size, extras, hidden, pad),
        out_shape=[shape(full, BF) for full in grads]
        + [shape((own, width), BF), shape((own, width), BF), shape((8, width), F32)],
        in_specs=[ANY, INNER] + [ANY] * 8 + [INNER, INNER, ANY],
        out_specs=[ANY] * 11,
        scratch_shapes=[
            vmem((own, width)), vmem((tokens, 1), F32), vmem((tokens, width)), vmem((width, tokens)),
            vmem((2, 4, width, local)), vmem((2, local, width)), vmem((2, 2 * hidden, width)),
            vmem((2, hidden, width)),
        ]
        + [vmem(heads)] * 9
        + [vmem((tokens, tokens))] * 2
        + [vmem(state)] * 4
        + [vmem((own, width))] * 4
        + [vmem((own, width), F32)] * 2
        + [
            vmem((tokens, width)), vmem((tokens, width)), vmem((2, tokens, 3 * pad)), vmem((own, width), F32),
            vmem(heads), vmem((2, 4, tokens, local)),
        ]
        + [vmem((tokens, local), F32)] * 3
        + [vmem((bits + 3, 8, width), F32), vmem((bits + 2, 8, width), F32)]
        + [vmem((2, hidden, width))] * 3
        + [vmem((2, local, width))]
        + received
        + [pltpu.SemaphoreType.DMA((copies,))] * 2
        + [
            pltpu.SemaphoreType.DMA((40,)), pltpu.SemaphoreType.REGULAR,
            pltpu.SemaphoreType.REGULAR((max(1, 12 * extras),)),
        ],
        compiler_params=pltpu.CompilerParams(collective_id=0, has_side_effects=True, vmem_limit_bytes=63 << 20),
    )(
        inputs, segments, query_weight, key_weight, value_weight, gate_weight, out_weight, left_weight.T,
        right_weight.T, down_weight, norm_first.reshape(1, -1), norm_second.reshape(1, -1), cotangent,
    )
    count, passed = len(grads), 3
    wide = pl.pallas_call(
        functools.partial(widen_kernel, count, passed),
        out_shape=[shape(full, F32) for full in grads] + [shape(r.shape, r.dtype) for r in results[count:]],
        in_specs=[ANY] * (count + passed),
        out_specs=[ANY] * (count + passed),
        scratch_shapes=[vmem(full) for full in grads]
        + [vmem(full, F32) for full in grads]
        + [pltpu.SemaphoreType.DMA((count,)), pltpu.SemaphoreType.DMA((count + passed,))],
        compiler_params=pltpu.CompilerParams(vmem_limit_bytes=48 << 20),
    )(*results)
    down, left, right, out, query, key, value, gate, block, block_grad, gains = wide
    return (
        block, block_grad, query, key, value, gate, out, left.T, right.T, down, gains[1], gains[0],
    )


def solution(mesh):
    row, column = P("tensor", None), P(None, "tensor")
    tokens = P(("dp", "tensor"), None)
    return jax.shard_map(
        functools.partial(per_device, mesh.shape["dp"]),
        mesh=mesh,
        in_specs=(
            tokens, P("dp", None), column, column, column, column, row, column, column, row, P(), P(), tokens,
        ),
        out_specs=(tokens, tokens, column, column, column, column, row, column, column, row, P(), P()),
        check_vma=False,
    )
```

time: 288 us -> 241 us (0.84)
  Pallas kernels: 265 us -> 229 us
  other arithmetic: 8.31 us -> 0 us
  local copies, waits for them, and re-layouts: 12.9 us -> 10 us
    pallas_call x2, Pallas kernels: 265 us -> 229 us  [the longest x1 222 us: per_device(): pl.pallas_call(functools.partial(layer_kernel, dp_size, extras, hidden, p...]
    convert_element_type x6 -> x0, other arithmetic: 8.31 us -> none  [per_device(): a.astype(F32)]
    unnamed x26 -> x18, local copies, waits for them, and re-layouts: 9.75 us -> 9.4 us
where the time goes in v3:
time: 241 us; the launch traced here: 240 us
  Pallas kernels  229 us (95%)
  local copies, waits for them, and re-layouts  10 us (4%)
    pallas_call x1, Pallas kernels, per_device(): pl.pallas_call(functools.partial(layer_kernel, dp_size, extras, hidden, p...  222 us
    unnamed x18, local copies, waits for them, and re-layouts  9.4 us
    pallas_call x1, Pallas kernels, per_device(): pl.pallas_call(functools.partial(widen_kernel, count, passed), out_shape=...  7.23 us

profile of v3, /device:TPU:0, one launch (start us, length us, event | category | flops | bytes accessed | tf_op | source)
XLA Modules:
  0.0 240.1 jit_solution(15332921020174756225)
XLA Ops:
  0.6 222.2 %shard_map.220 = (bf16[704,1024]{1,0:T(8,128)(2,1)}, bf16[704,1024]{1,0:T(8,128)(2,1)}, bf16[704,1024]{1,0:T(8,128)(2,1)}, bf16[256,1024]{1,0:T(8,128)(2,1)}, bf...) custom-call(bf16[256,1024]{1,0:T(8,128)(2,1)} %x_hbm.1, ...), custom_call_target="tpu_custom_call" | custom-call | tf_op jit(solution)/shard_map/pallas_call | solution.py:789
  222.8 0.0 copy-start
  222.8 1.4 copy-done
  224.2 0.0 copy-start.1
  224.2 1.0 copy-done.1
  225.2 0.0 copy-start.2
  225.2 1.0 copy-done.2
  226.3 0.0 copy-start.3
  226.3 1.0 copy-done.3
  227.3 0.0 copy-start.4
  227.3 1.0 copy-done.4
  228.3 0.0 copy-start.5
  228.4 1.0 copy-done.5
  229.4 0.0 copy-start.6
  229.4 1.0 copy-done.6
  230.4 0.0 copy-start.7
  230.4 1.0 copy-done.7
  231.5 0.0 copy-start.8
  231.5 0.8 copy-done.8
  232.2 7.2 %shard_map.221 = (f32[704,1024]{1,0:T(8,128)}, f32[704,1024]{1,0:T(8,128)}, f32[704,1024]{1,0:T(8,128)}, f32[256,1024]{1,0:T(8,128)}, f32[1024,256]{1,0:T(8,128)...) custom-call(bf16[704,1024]{1,0:T(8,128)(2,1)S(1)} %copy-done, ...), custom_call_target="tpu_custom_call" | custom-call | tf_op jit(solution)/shard_map/pallas_call | solution.py:825
  239.5 0.6 fusion
Async XLA Ops:
  222.8 1.4 copy-start
  224.2 1.0 copy-start.1
  225.2 1.0 copy-start.2
  226.3 1.0 copy-start.3
  227.3 1.0 copy-start.4
  228.3 1.0 copy-start.5
  229.4 1.0 copy-start.6
  230.4 1.0 copy-start.7
  231.5 0.8 copy-start.8

commit v4 on v3

--- a/solution.py
+++ b/solution.py
@@ -33,6 +33,8 @@
         self.half = lax.rem(self.t, 2)
         self.pair = self.t // 2
         self.bits = dp_size.bit_length() - 1
+        self.rows = [{"dp": lax.rem(self.i + k, dp_size)} for k in range(1, dp_size)]
+        self.columns = [{"tensor": lax.rem(self.t + k, 4)} for k in range(1, 4)]
         self.mate = {"tensor": self.t + 1 - 2 * self.half}
         self.twin = {"tensor": self.t + 2 - 4 * self.pair}
 
@@ -44,7 +46,7 @@
 
     def greet(self):
         barrier = pltpu.get_barrier_semaphore()
-        peers = [self.mate, self.twin] + [self.over(b) for b in range(self.bits)]
+        peers = self.rows + self.columns
         for peer in peers:
             pl.semaphore_signal(barrier, inc=1, device_id=peer, device_id_type=MESH)
 
@@ -186,7 +188,7 @@
 
 
 class Reduce:
-    def __init__(self, place, links, moves, grad, axis, order, halves, credits, twin_recv, out):
+    def __init__(self, place, links, moves, grad, axis, order, halves, credits, twin_recv, out, other=None):
         self.place, self.links, self.moves = place, links, moves
         self.grad, self.axis, self.order = grad, axis, order
         self.halves, self.twin_recv, self.out = halves, twin_recv, out
@@ -194,7 +196,8 @@
         self.size = grad.shape[1 + axis] // (1 << len(order))
         self.piece = piece_of(place, order)
         self.stage, self.copy, self.local = 0, None, None
-        self.steps = len(order) + len(self.extra) + 1 + len(order)
+        self.other, self.ends = other, out is None
+        self.steps = len(order) + len(self.extra) + (0 if self.ends else 1 + len(order))
 
     def first_of(self, width):
         return pl.multiple_of((self.piece // width) * (width * self.size), self.size)
@@ -226,8 +229,13 @@
             return
         k -= len(self.extra)
         if k == 0:
-            source = self.grad_part((1,), self.first_of(1), 1)
-            self.copy = self.links.start(source, self.twin_recv, self.place.twin)
+            if self.other is not None:
+                while not self.other.over():
+                    self.other.advance()
+                self.copy = self.other.copy
+            else:
+                source = self.grad_part((self.grad.shape[0] - 1,), self.first_of(1), 1)
+                self.copy = self.links.start(source, self.twin_recv, self.place.twin)
             return
         k -= 1
         block = self.out_part(1 << k)
@@ -268,7 +276,7 @@
             self.moves.wait(self.local)
             self.local = None
         self.stage += 1
-        if self.stage < self.steps:
+        if self.stage < self.steps or self.ends:
             self.begin()
 
     def over(self):
@@ -366,83 +374,101 @@
                 (sq, sk)[j][shard, at, :] = slope.astype(BF)
 
     project(0, mine, (1, 2, 0, 3))
+    across, last = marks_of(place, segr_ref, segc, tokens)
+    doc_mask(across, segc, mask, tokens, False)
+    near = segc[...] == last
+    state_copy = [None, None]
+
+    def send_state(shard):
+        keys = jnp.where(near, kp[shard].astype(F32), 0.0).astype(BF)
+        state_send[shard] = fold(dot(keys.T, vl[shard]))
+        state_copy[shard] = links.start(state_send.at[shard], state_recv.at[1 - shard], place.twin)
+
+    attention = (join_a, join_b, gather_o)
+    normed_copy.wait_recv()
+    advance(*attention)
     for copy in ffn_in:
         moves.wait(copy)
     gather_l.begin()
     gather_r.begin()
     gather_d.begin()
-    across, last = marks_of(place, segr_ref, segc, tokens)
-    doc_mask(across, segc, mask, tokens, False)
+    project(0, theirs, (1, 2))
+    send_state(0)
+    advance(*attention)
     moves.wait(cot_in)
-    normed_copy.wait_recv()
     cot_block = cot.at[pl.ds(mine, own), :]
     cot_copy = links.start(cot_block, cot_block, place.mate)
-    project(0, theirs, (1, 2))
-    near = segc[...] == last
-    state_copy = [None, None]
-
-    def send_state(shard):
-        keys = jnp.where(near, kp[shard].astype(F32), 0.0).astype(BF)
-        state_send[shard] = fold(dot(keys.T, vl[shard]))
-        state_copy[shard] = links.start(state_send.at[shard], state_recv.at[1 - shard], place.twin)
-
-    send_state(0)
     project(0, theirs, (0, 3))
-    advance(join_a, join_b, gather_o)
-
-    def mix(shard):
+
+    def mix(shard, total):
         def one(head, carry):
             for r in range(2):
                 seen = (r + 1) * own
                 at = slice(r * own, (r + 1) * own)
                 raw = dot_t(only_head(qp[shard, at, :], head), kp[shard, :seen, :])
                 scores = raw.astype(BF) * mask[at, :seen]
-                dq[at, :] += dot(scores, only_head(vl[shard, :seen, :], head))
+                total[at, :] += dot(scores, only_head(vl[shard, :seen, :], head))
             return carry
 
-        dq[...] = jnp.zeros(dq.shape, F32)
+        total[...] = jnp.zeros(total.shape, F32)
         lax.fori_loop(0, local // HEAD, one, 0)
 
     first_half, second_half = place.pair == 0, place.pair == 1
 
-    def open_gate(shard):
+    def open_gate(shard, total):
         state_copy[1 - shard].wait_recv()
         query = jnp.where(near & second_half, qp[shard].astype(F32), 0.0).astype(BF)
-        mixed = dq[...] + dot(query, unfold(state_recv[shard]))
+        mixed = total[...] + dot(query, unfold(state_recv[shard]))
         scale = lax.rsqrt(head_mean(mixed * mixed) + EPS)
         norm = mixed * scale
         rr[shard] = scale.astype(BF)
         hn[shard] = norm.astype(BF)
         gated[shard] = (norm * sz[shard].astype(F32)).astype(BF)
 
-    mix(0)
-    advance(join_a, join_b, gather_o, gather_l)
-    advance(join_a, join_b, gather_o, gather_r, gather_l)
-    advance(join_a, join_b, gather_o)
+    mix(0, dk)
+    advance(*attention)
+    advance(gather_l)
+    advance(*attention)
     for first in (mine, theirs):
         project(1, first, (1, 2))
     send_state(1)
-    open_gate(0)
-    advance(gather_d, gather_r, gather_l)
+    advance(gather_r)
     for first in (mine, theirs):
         project(1, first, (0, 3))
-    advance(gather_d, gather_r, gather_l)
-    mix(1)
+    advance(gather_l, gather_d)
+    mix(1, dq)
+    advance(gather_r, gather_l)
+    open_gate(1, dq)
+    open_gate(0, dk)
+
+    def branch(first, count=own):
+        at = pl.ds(first, count)
+        return dot(gated[0, at, :], ow[0]) + dot(gated[1, at, :], ow[1])
+
+    part_rows = own // 2
+    parts = [slice(0, part_rows), slice(part_rows, own)]
+
+    def halved(partial_sum, send, recv):
+        copies = []
+        for rows in parts:
+            send[rows, :] = partial_sum(pl.multiple_of(theirs + rows.start, part_rows), part_rows).astype(BF)
+            copies.append(links.start(send.at[rows, :], recv.at[rows, :], place.mate))
+        return copies
+
+    def share(ref):
+        def after(n):
+            block = ref.at[pl.ds(pl.multiple_of(mine + n * part_rows, part_rows), part_rows), :]
+            return links.start(block, block, place.mate)
+
+        return after
+
+    branch_copies = halved(branch, trade_send, trade_recv)
+    own_sum[...] = branch(mine)
     advance(gather_d, gather_r)
-    open_gate(1)
-
-    def branch(first):
-        at = pl.ds(first, own)
-        return dot(gated[0, at, :], ow[0]) + dot(gated[1, at, :], ow[1])
-
-    trade_send[...] = branch(theirs).astype(BF)
-    branch_copy = links.start(trade_send, trade_recv, place.mate)
-    own_sum[...] = branch(mine)
-    advance(gather_d)
     for c in range(0, width, 256):
         normed_t[c : c + 256, :] = normed[:, c : c + 256].T
     doc_mask(across, segc, mask_t, tokens, True)
-    branch_copy.wait_recv()
+    advance(gather_d, gather_l, gather_r)
 
     def second_norm(first):
         at = pl.ds(first, 32)
@@ -451,10 +477,13 @@
         scale = lax.rsqrt(jnp.mean(values * values, axis=-1, keepdims=True) + EPS)
         second[pl.ds(mine + first, 32), :] = (values * scale * g2_ref[...]).astype(BF)
 
-    rows_loop(own, 32, second_norm)
-    block = second.at[pl.ds(mine, own), :]
-    second_copy = links.start(block, block, place.mate)
+    second_copies = []
+    for n, copy in enumerate(branch_copies):
+        copy.wait_recv()
+        rows_loop(part_rows, 32, lambda first, n=n: second_norm(pl.multiple_of(n * part_rows + first, 32)))
+        second_copies.append(share(second)(n))
     cot_copy.wait_recv()
+    advance(gather_d)
 
     def hidden_grad(first):
         at = pl.ds(first, own)
@@ -482,11 +511,12 @@
     hidden_grad(mine)
     unit_rows(mine)
     hidden_grad(theirs)
-    second_copy.wait_recv()
+    for copy in second_copies:
+        copy.wait_recv()
     unit_rows(theirs)
 
-    def back(first):
-        at = pl.ds(first, own)
+    def back(first, count=own):
+        at = pl.ds(first, count)
         return (
             dot(hid[0, at, dleft], lw[0])
             + dot(hid[0, at, dright], rw[0])
@@ -498,17 +528,17 @@
         at = pl.ds(first, own)
         return dot(hid[0, at, product], dw[0]) + dot(hid[1, at, product], dw[1])
 
-    back_send[...] = back(theirs).astype(BF)
-    back_copy = links.start(back_send, back_recv, place.mate)
+    back_copies = halved(back, back_send, back_recv)
     own_sum[...] = back(mine)
 
-    def make_unit(grad, axis, order, out, first_half_ref=None):
+    def make_unit(grad, axis, order, out, first_half_ref=None, twin_recv=None, other=None):
         folds = len(order)
         halves = [received.pop(0) for _ in range(folds - (first_half_ref is not None))]
         if first_half_ref is not None:
             halves = [first_half_ref] + halves
         credits = [credit_sem.at[next(tickets)] for _ in range(extras)]
-        return Reduce(place, links, moves, grad, axis, order, halves, credits, received.pop(0), out)
+        twin_recv = received.pop(0) if twin_recv is None else twin_recv
+        return Reduce(place, links, moves, grad, axis, order, halves, credits, twin_recv, out, other)
 
     def split_units(grad, out):
         rows = grad.shape[1] // 2
@@ -521,18 +551,18 @@
         split_units(g, o) for g, o in ((grad_d, down_out), (grad_l, left_out), (grad_r, right_out))
     )
     ow_units = split_units(grad_o, ow_out)
-    joined_units = [
-        make_unit(
-            lrw.at[:, :width, j * local : (j + 1) * local], 0, order, out,
-            hid.at[:, : width // 2, j * local : (j + 1) * local],
-        )
-        for j, (order, out) in enumerate(
-            zip(
-                (first_order, second_order, first_order, second_order),
-                (query_out, key_out, value_out, gate_out),
-            )
-        )
-    ]
+    joined_units = []
+    for j, (order, out) in enumerate(
+        zip((first_order, second_order, first_order, second_order), (query_out, key_out, value_out, gate_out))
+    ):
+        columns = slice(j * local, (j + 1) * local)
+        grad, landing = lrw.at[:, :width, columns], hid.at[:, : width // 2, columns]
+        if j == 3:
+            joined_units.append(make_unit(grad, 0, order, out, landing))
+            continue
+        away = make_unit(grad.at[1:2], 0, order, None, landing.at[1:2])
+        near_unit = make_unit(grad.at[0:1], 0, order, out, landing.at[0:1], away.twin_recv, away)
+        joined_units.append((near_unit, away))
     live = []
 
     def launch(*units):
@@ -557,8 +587,9 @@
     hidden_outer(down_units, grad_d, product, cot)
     hidden_outer(left_units, grad_l, dleft, second)
     advance(*down_units)
-    back_copy.wait_recv()
-
+    hidden_outer(right_units, grad_r, dright, second)
+    advance(*left_units)
+    pl.semaphore_signal(free_sem, inc=1, device_id=place.over(0), device_id_type=MESH)
     gains[0] = jnp.zeros(gains.shape[1:], F32)
 
     def residual_back(first):
@@ -575,22 +606,22 @@
         dres_all[pl.ds(mine + first, 32), :] = total.astype(BF)
 
     links.settle(normed_copy)
-    rows_loop(own, 32, residual_back)
-    block = dres_all.at[pl.ds(mine, own), :]
-    dres_copy = links.start(block, block, place.mate)
-    hidden_outer(right_units, grad_r, dright, second)
-    advance(*left_units)
-    links.settle(back_copy)
+    dres_copies = []
+    for n, copy in enumerate(back_copies):
+        copy.wait_recv()
+        rows_loop(part_rows, 32, lambda first, n=n: residual_back(pl.multiple_of(n * part_rows + first, 32)))
+        dres_copies.append(share(dres_all)(n))
+    advance(*right_units)
+    links.settle(*back_copies)
     back_send[...] = ffn(theirs).astype(BF)
 
     def add_ffn(first):
         resid[...] += ffn(first)
 
     add_ffn(mine)
-    advance(*right_units)
-    pl.semaphore_signal(free_sem, inc=1, device_id=place.over(0), device_id_type=MESH)
     advance(*down_units)
-    dres_copy.wait_recv()
+    for copy in dres_copies:
+        copy.wait_recv()
     ffn_copy = links.start(back_send, back_recv, place.mate)
 
     def gate_back(shard, carry):
@@ -619,19 +650,16 @@
         links.settle(*unit.sent)
     pl.semaphore_wait(free_sem, 1)
 
-    def project_back(j):
+    def project_back(j, shard):
         def body(first):
-            def one(shard, carry):
-                part_grad = dot(normed_t[pl.ds(first, 256), :], djoined[shard, j])
-                lrw[shard, pl.ds(first, 256), j * local : (j + 1) * local] = part_grad.astype(BF)
-                return carry
-
-            lax.fori_loop(0, 2, one, 0)
+            part_grad = dot(normed_t[pl.ds(first, 256), :], djoined[shard, j])
+            lrw[shard, pl.ds(first, 256), j * local : (j + 1) * local] = part_grad.astype(BF)
 
         rows_loop(width, 256, body)
-        launch(joined_units[j])
-
-    project_back(3)
+
+    project_back(3, 0)
+    project_back(3, 1)
+    launch(joined_units[3])
     step_all()
 
     def mix_back(shard):
@@ -657,10 +685,8 @@
 
         lax.fori_loop(0, local // HEAD, one, 0)
 
-    for shard in range(2):
+    for shard in (1, 0):
         mix_back(shard)
-        if shard == 0:
-            step_all()
         meets[1 - shard].wait_recv()
         meet = unfold(meet_recv[shard])
         marks = near & first_half
@@ -668,11 +694,11 @@
         from_meet = jnp.where(marks, dot_t(vl[shard], meet), 0.0)
         djoined[shard, 1] = ((dk[...] + from_meet) * sk[shard].astype(F32)).astype(BF)
         djoined[shard, 0] = (dq[...] * sq[shard].astype(F32)).astype(BF)
-
-    project_back(0)
-    project_back(1)
-    project_back(2)
-    step_all()
+        if shard == 1:
+            step_all()
+        for j in range(3):
+            project_back(j, shard)
+            launch(joined_units[j][shard])
 
     def normed_back(first):
         at = pl.ds(first, own)
@@ -684,7 +710,7 @@
 
         lax.fori_loop(0, 8, one, 0)
 
-    links.settle(branch_copy)
+    links.settle(*branch_copies)
     normed_back(theirs)
     trade_send[...] = own_sum[...].astype(BF)
     trade_copy = links.start(trade_send, trade_recv, place.mate)
@@ -716,13 +742,15 @@
     rows_loop(own, 32, finish_grad)
     moves.start(trade_send, grad_out)
 
-    peers = [place.over(b) for b in range(place.bits)] + [place.mate, place.twin]
-    for n, peer in enumerate(peers):
-        copy = links.start(gains.at[n], gains_recv.at[n], peer)
+    first = 0
+    for n, peers in enumerate((place.rows, place.columns)):
+        copies = [links.start(gains.at[n], gains_recv.at[first + k], peer) for k, peer in enumerate(peers)]
         step_all()
-        copy.wait_recv()
-        gains[n + 1] = gains[n] + gains_recv[n]
-    moves.start(gains.at[len(peers)], gains_out)
+        for copy in copies:
+            copy.wait_recv()
+        gains[n + 1] = gains[n] + jnp.sum(gains_recv[first : first + len(peers)], axis=0)
+        first += len(peers)
+    moves.start(gains.at[2], gains_out)
     while not all(unit.over() for unit in live):
         step_all()
     moves.finish()
@@ -732,13 +760,12 @@
 def widen_kernel(count, passed, *refs):
     sources, refs = refs[: count + passed], refs[count + passed :]
     targets, refs = refs[: count + passed], refs[count + passed :]
-    narrow, wide, (in_sem, out_sem) = refs[:count], refs[count : 2 * count], refs[2 * count :]
-    loads = [pltpu.make_async_copy(sources[n], narrow[n], in_sem.at[n]) for n in range(count)]
-    stores = [pltpu.make_async_copy(wide[n], targets[n], out_sem.at[n]) for n in range(count)]
-    stores += [
-        pltpu.make_async_copy(sources[n], targets[n], out_sem.at[n]) for n in range(count, count + passed)
-    ]
-    for copy in loads + stores[count:]:
+    total = count + passed
+    narrow, wide, (in_sem, out_sem) = refs[:total], refs[total : total + count], refs[total + count :]
+    loads = [pltpu.make_async_copy(sources[n], narrow[n], in_sem.at[n]) for n in range(total)]
+    results = list(wide) + list(narrow[count:])
+    stores = [pltpu.make_async_copy(results[n], targets[n], out_sem.at[n]) for n in range(total)]
+    for copy in loads:
         copy.start()
     for n in range(count):
         loads[n].wait()
@@ -747,6 +774,9 @@
             wide[n][pl.ds(first, 64), :] = narrow[n][pl.ds(first, 64), :].astype(F32)
 
         rows_loop(narrow[n].shape[0], 64, body)
+        stores[n].start()
+    for n in range(count, total):
+        loads[n].wait()
         stores[n].start()
     for copy in stores:
         copy.wait()
@@ -772,9 +802,9 @@
     heads, state = (2, tokens, local), (2, local, local // 2)
     grads = [(hidden, width)] * 3 + [(local, width)] + [(width, local)] * 4
 
-    def buffers(rows, columns, axis, first):
+    def buffers(rows, columns, axis, first, shards=2):
         def cut(parts):
-            return (2, rows // parts, columns) if axis == 0 else (2, rows, columns // parts)
+            return (shards, rows // parts, columns) if axis == 0 else (shards, rows, columns // parts)
 
         eighth = cut(1 << PIECE_BITS)
         kept = [vmem(cut(2 << k)) for k in range(first, PIECE_BITS)]
@@ -783,13 +813,15 @@
     received = []
     for rows in (hidden // 2,) * 6 + (local // 2,) * 2:
         received += buffers(rows, width, 1, 0)
-    for _ in range(4):
-        received += buffers(width, local, 0, 1)
-    copies = 12 * (2 * PIECE_BITS + extras + 1) + 6 * (PIECE_BITS + 1) + bits + 16
+    for _ in range(3):
+        away = buffers(width, local, 0, 1, 1)
+        received += away + away[:-1]
+    received += buffers(width, local, 0, 1)
+    copies = 15 * (2 * PIECE_BITS + extras + 1) + 6 * (PIECE_BITS + 1) + dp_size + 20
     results = pl.pallas_call(
         functools.partial(layer_kernel, dp_size, extras, hidden, pad),
         out_shape=[shape(full, BF) for full in grads]
-        + [shape((own, width), BF), shape((own, width), BF), shape((8, width), F32)],
+        + [shape((own, width), BF), shape((own, width), BF), shape((2, width), F32)],
         in_specs=[ANY, INNER] + [ANY] * 8 + [INNER, INNER, ANY],
         out_specs=[ANY] * 11,
         scratch_shapes=[
@@ -807,14 +839,14 @@
             vmem(heads), vmem((2, 4, tokens, local)),
         ]
         + [vmem((tokens, local), F32)] * 3
-        + [vmem((bits + 3, 8, width), F32), vmem((bits + 2, 8, width), F32)]
+        + [vmem((3, 2, width), F32), vmem((dp_size + 2, 2, width), F32)]
         + [vmem((2, hidden, width))] * 3
         + [vmem((2, local, width))]
         + received
         + [pltpu.SemaphoreType.DMA((copies,))] * 2
         + [
             pltpu.SemaphoreType.DMA((40,)), pltpu.SemaphoreType.REGULAR,
-            pltpu.SemaphoreType.REGULAR((max(1, 12 * extras),)),
+            pltpu.SemaphoreType.REGULAR((max(1, 15 * extras),)),
         ],
         compiler_params=pltpu.CompilerParams(collective_id=0, has_side_effects=True, vmem_limit_bytes=63 << 20),
     )(
@@ -827,10 +859,10 @@
         out_shape=[shape(full, F32) for full in grads] + [shape(r.shape, r.dtype) for r in results[count:]],
         in_specs=[ANY] * (count + passed),
         out_specs=[ANY] * (count + passed),
-        scratch_shapes=[vmem(full) for full in grads]
+        scratch_shapes=[vmem(r.shape, r.dtype) for r in results]
         + [vmem(full, F32) for full in grads]
-        + [pltpu.SemaphoreType.DMA((count,)), pltpu.SemaphoreType.DMA((count + passed,))],
-        compiler_params=pltpu.CompilerParams(vmem_limit_bytes=48 << 20),
+        + [pltpu.SemaphoreType.DMA((count + passed,))] * 2,
+        compiler_params=pltpu.CompilerParams(vmem_limit_bytes=62 << 20),
     )(*results)
     down, left, right, out, query, key, value, gate, block, block_grad, gains = wide
     return (

time: 241 us -> 222 us (0.921)
  Pallas kernels: 229 us -> 220 us
  local copies, waits for them, and re-layouts: 10 us -> 1.38 us
    pallas_call x1, Pallas kernels: 222 us -> 212 us  [per_device(): pl.pallas_call(functools.partial(layer_kernel, dp_size, extras, hidden, p...]
    unnamed x18 -> x0, local copies, waits for them, and re-layouts: 9.4 us -> none
where the time goes in v4:
time: 222 us
  Pallas kernels  220 us (99%)
    pallas_call x1, Pallas kernels, per_device(): pl.pallas_call(functools.partial(layer_kernel, dp_size, extras, hidden, p...  212 us
    pallas_call x1, Pallas kernels, per_device(): pl.pallas_call(functools.partial(widen_kernel, count, passed), out_shape=...  7.4 us

profile of v4, /device:TPU:0, one launch (start us, length us, event | category | flops | bytes accessed | tf_op | source)
XLA Modules:
  0.0 221.6 jit_solution(3435866633905749554)
XLA Ops:
  0.6 212.1 %shard_map.220 = (bf16[704,1024]{1,0:T(8,128)(2,1)}, bf16[704,1024]{1,0:T(8,128)(2,1)}, bf16[704,1024]{1,0:T(8,128)(2,1)}, bf16[256,1024]{1,0:T(8,128)(2,1)}, bf...) custom-call(bf16[256,1024]{1,0:T(8,128)(2,1)} %x_hbm.1, ...), custom_call_target="tpu_custom_call" | custom-call | tf_op jit(solution)/shard_map/pallas_call | solution.py:821
  212.8 7.4 %shard_map.221 = (f32[704,1024]{1,0:T(8,128)}, f32[704,1024]{1,0:T(8,128)}, f32[704,1024]{1,0:T(8,128)}, f32[256,1024]{1,0:T(8,128)}, f32[1024,256]{1,0:T(8,128)...) custom-call(bf16[704,1024]{1,0:T(8,128)(2,1)} %get-tuple-element.34., ...), custom_call_target="tpu_custom_call" | custom-call | tf_op jit(solution)/shard_map/pallas_call | solution.py:857
  220.2 1.4 fusion

commit v5 on v4

--- a/solution.py
+++ b/solution.py
@@ -435,9 +435,9 @@
     advance(gather_r)
     for first in (mine, theirs):
         project(1, first, (0, 3))
-    advance(gather_l, gather_d)
+    advance(gather_l)
     mix(1, dq)
-    advance(gather_r, gather_l)
+    advance(gather_r)
     open_gate(1, dq)
     open_gate(0, dk)
 
@@ -463,8 +463,9 @@
         return after
 
     branch_copies = halved(branch, trade_send, trade_recv)
+    advance(gather_d, gather_l)
     own_sum[...] = branch(mine)
-    advance(gather_d, gather_r)
+    advance(gather_r, gather_d)
     for c in range(0, width, 256):
         normed_t[c : c + 256, :] = normed[:, c : c + 256].T
     doc_mask(across, segc, mask_t, tokens, True)
@@ -570,8 +571,8 @@
             unit.begin()
             live.append(unit)
 
-    def step_all():
-        for unit in live:
+    def step_all(late=False):
+        for unit in reversed(live) if late else live:
             unit.advance()
 
     def hidden_outer(units, grad, left, right):
@@ -694,8 +695,6 @@
         from_meet = jnp.where(marks, dot_t(vl[shard], meet), 0.0)
         djoined[shard, 1] = ((dk[...] + from_meet) * sk[shard].astype(F32)).astype(BF)
         djoined[shard, 0] = (dq[...] * sq[shard].astype(F32)).astype(BF)
-        if shard == 1:
-            step_all()
         for j in range(3):
             project_back(j, shard)
             launch(joined_units[j][shard])
@@ -714,7 +713,7 @@
     normed_back(theirs)
     trade_send[...] = own_sum[...].astype(BF)
     trade_copy = links.start(trade_send, trade_recv, place.mate)
-    step_all()
+    step_all(True)
     normed_back(mine)
     ffn_copy.wait_recv()
     links.settle(ffn_copy)
@@ -725,7 +724,7 @@
 
     rows_loop(own, 32, finish_out)
     moves.start(back_send, block_out)
-    step_all()
+    step_all(True)
     trade_copy.wait_recv()
     links.settle(trade_copy)
 
@@ -745,14 +744,14 @@
     first = 0
     for n, peers in enumerate((place.rows, place.columns)):
         copies = [links.start(gains.at[n], gains_recv.at[first + k], peer) for k, peer in enumerate(peers)]
-        step_all()
+        step_all(True)
         for copy in copies:
             copy.wait_recv()
         gains[n + 1] = gains[n] + jnp.sum(gains_recv[first : first + len(peers)], axis=0)
         first += len(peers)
     moves.start(gains.at[2], gains_out)
     while not all(unit.over() for unit in live):
-        step_all()
+        step_all(True)
     moves.finish()
     links.finish()
 

time: 222 us -> 210 us (0.946)
  Pallas kernels: 220 us -> 206 us
    pallas_call x1, Pallas kernels: 212 us -> 198 us  [per_device(): pl.pallas_call(functools.partial(layer_kernel, dp_size, extras, hidden, p...]
where the time goes in v5:
time: 210 us; the launch traced here: 208 us
  Pallas kernels  206 us (98%)
    pallas_call x1, Pallas kernels, per_device(): pl.pallas_call(functools.partial(layer_kernel, dp_size, extras, hidden, p...  198 us
    pallas_call x1, Pallas kernels, per_device(): pl.pallas_call(functools.partial(widen_kernel, count, passed), out_shape=...  7.4 us

profile of v5, /device:TPU:0, one launch (start us, length us, event | category | flops | bytes accessed | tf_op | source)
XLA Modules:
  0.0 207.8 jit_solution(12572554189589282066)
XLA Ops:
  0.6 198.4 %shard_map.220 = (bf16[704,1024]{1,0:T(8,128)(2,1)}, bf16[704,1024]{1,0:T(8,128)(2,1)}, bf16[704,1024]{1,0:T(8,128)(2,1)}, bf16[256,1024]{1,0:T(8,128)(2,1)}, bf...) custom-call(bf16[256,1024]{1,0:T(8,128)(2,1)} %x_hbm.1, ...), custom_call_target="tpu_custom_call" | custom-call | tf_op jit(solution)/shard_map/pallas_call | solution.py:820
  199.0 7.4 %shard_map.221 = (f32[704,1024]{1,0:T(8,128)}, f32[704,1024]{1,0:T(8,128)}, f32[704,1024]{1,0:T(8,128)}, f32[256,1024]{1,0:T(8,128)}, f32[1024,256]{1,0:T(8,128)...) custom-call(bf16[704,1024]{1,0:T(8,128)(2,1)} %get-tuple-element.34., ...), custom_call_target="tpu_custom_call" | custom-call | tf_op jit(solution)/shard_map/pallas_call | solution.py:856
  206.5 1.4 fusion

commit v6 on v5

--- a/solution.py
+++ b/solution.py
@@ -377,7 +377,18 @@
     across, last = marks_of(place, segr_ref, segc, tokens)
     doc_mask(across, segc, mask, tokens, False)
     near = segc[...] == last
+    edge = segc[...] == segc[own - 1 : own, :]
+    halves_of = (slice(0, own), slice(own, tokens))
     state_copy = [None, None]
+
+    def marked(values, marks):
+        return jnp.where(marks, values.astype(F32), 0.0).astype(BF)
+
+    def blocks(left, right):
+        return jnp.where(same_head(local), dot(left.T, right), 0.0).astype(BF)
+
+    def middle_state(shard):
+        return blocks(marked(kp[shard, :own, :], edge[:own]), vl[shard, :own, :])
 
     def send_state(shard):
         keys = jnp.where(near, kp[shard].astype(F32), 0.0).astype(BF)
@@ -402,15 +413,14 @@
 
     def mix(shard, total):
         def one(head, carry):
-            for r in range(2):
-                seen = (r + 1) * own
-                at = slice(r * own, (r + 1) * own)
-                raw = dot_t(only_head(qp[shard, at, :], head), kp[shard, :seen, :])
-                scores = raw.astype(BF) * mask[at, :seen]
-                total[at, :] += dot(scores, only_head(vl[shard, :seen, :], head))
+            for at in halves_of:
+                raw = dot_t(only_head(qp[shard, at, :], head), kp[shard, at, :])
+                scores = raw.astype(BF) * mask[at, at]
+                total[at, :] += dot(scores, only_head(vl[shard, at, :], head))
             return carry
 
-        total[...] = jnp.zeros(total.shape, F32)
+        total[:own, :] = jnp.zeros((own, local), F32)
+        total[own:, :] = dot(marked(qp[shard, own:, :], edge[own:]), middle_state(shard))
         lax.fori_loop(0, local // HEAD, one, 0)
 
     first_half, second_half = place.pair == 0, place.pair == 1
@@ -665,23 +675,25 @@
 
     def mix_back(shard):
         dq[...] = jnp.where(near & second_half, dot_t(dm[shard], unfold(state_recv[shard])), 0.0)
-        dk[...] = jnp.zeros(dk.shape, F32)
-        dv[...] = jnp.zeros(dv.shape, F32)
+        dq[own:, :] += jnp.where(edge[own:], dot_t(dm[shard, own:, :], middle_state(shard)), 0.0)
+        meeting = blocks(marked(qp[shard, own:, :], edge[own:]), dm[shard, own:, :])
+        dk[:own, :] = jnp.where(edge[:own], dot_t(vl[shard, :own, :], meeting), 0.0)
+        dv[:own, :] = jnp.where(edge[:own], dot(kp[shard, :own, :], meeting), 0.0)
+        dk[own:, :] = jnp.zeros((own, local), F32)
+        dv[own:, :] = jnp.zeros((own, local), F32)
 
         def one(head, carry):
-            for r in range(2):
-                seen = (r + 1) * own
-                at = slice(r * own, (r + 1) * own)
+            for at in halves_of:
                 grad_r, query_r = dm[shard, at, :], qp[shard, at, :]
                 grad_h, query_h = only_head(grad_r, head), only_head(query_r, head)
-                keys_h = only_head(kp[shard, :seen, :], head)
-                vals_h = only_head(vl[shard, :seen, :], head)
-                ds = dot_t(grad_r, vals_h).astype(BF) * mask[at, :seen]
+                keys_h = only_head(kp[shard, at, :], head)
+                vals_h = only_head(vl[shard, at, :], head)
+                ds = dot_t(grad_r, vals_h).astype(BF) * mask[at, at]
                 dq[at, :] += dot(ds, keys_h)
-                st = dot_t(keys_h, query_r).astype(BF) * mask_t[:seen, at]
-                dv[:seen, :] += dot(st, grad_h)
-                dst = dot_t(vals_h, grad_r).astype(BF) * mask_t[:seen, at]
-                dk[:seen, :] += dot(dst, query_h)
+                st = dot_t(keys_h, query_r).astype(BF) * mask_t[at, at]
+                dv[at, :] += dot(st, grad_h)
+                dst = dot_t(vals_h, grad_r).astype(BF) * mask_t[at, at]
+                dk[at, :] += dot(dst, query_h)
             return carry
 
         lax.fori_loop(0, local // HEAD, one, 0)

time: 210 us -> 209 us (level)
  no operation moved by 1% of the time
where the time goes in v6:
time: 209 us; the launch traced here: 208 us
  Pallas kernels  206 us (99%)
    pallas_call x1, Pallas kernels, per_device(): pl.pallas_call(functools.partial(layer_kernel, dp_size, extras, hidden, p...  199 us
    pallas_call x1, Pallas kernels, per_device(): pl.pallas_call(functools.partial(widen_kernel, count, passed), out_shape=...  7.4 us

profile of v6, /device:TPU:0, one launch (start us, length us, event | category | flops | bytes accessed | tf_op | source)
XLA Modules:
  0.0 208.3 jit_solution(9659284294372280304)
XLA Ops:
  0.6 198.9 %shard_map.220 = (bf16[704,1024]{1,0:T(8,128)(2,1)}, bf16[704,1024]{1,0:T(8,128)(2,1)}, bf16[704,1024]{1,0:T(8,128)(2,1)}, bf16[256,1024]{1,0:T(8,128)(2,1)}, bf...) custom-call(bf16[256,1024]{1,0:T(8,128)(2,1)} %x_hbm.1, ...), custom_call_target="tpu_custom_call" | custom-call | tf_op jit(solution)/shard_map/pallas_call | solution.py:832
  199.5 7.4 %shard_map.221 = (f32[704,1024]{1,0:T(8,128)}, f32[704,1024]{1,0:T(8,128)}, f32[704,1024]{1,0:T(8,128)}, f32[256,1024]{1,0:T(8,128)}, f32[1024,256]{1,0:T(8,128)...) custom-call(bf16[704,1024]{1,0:T(8,128)(2,1)} %get-tuple-element.34., ...), custom_call_target="tpu_custom_call" | custom-call | tf_op jit(solution)/shard_map/pallas_call | solution.py:868
  206.9 1.4 fusion

commit v7 on v6

--- a/solution.py
+++ b/solution.py
@@ -582,7 +582,7 @@
             live.append(unit)
 
     def step_all(late=False):
-        for unit in reversed(live) if late else live:
+        for unit in live[:6] + live[:5:-1] if late else live:
             unit.advance()
 
     def hidden_outer(units, grad, left, right):

time: 209 us -> 209 us (level)
  no operation moved by 1% of the time
where the time goes in v7:
time: 209 us
  Pallas kernels  207 us (99%)
    pallas_call x1, Pallas kernels, per_device(): pl.pallas_call(functools.partial(layer_kernel, dp_size, extras, hidden, p...  199 us
    pallas_call x1, Pallas kernels, per_device(): pl.pallas_call(functools.partial(widen_kernel, count, passed), out_shape=...  7.4 us

profile of v7, /device:TPU:0, one launch (start us, length us, event | category | flops | bytes accessed | tf_op | source)
XLA Modules:
  0.0 208.8 jit_solution(5923505700429280979)
XLA Ops:
  0.6 199.3 %shard_map.220 = (bf16[704,1024]{1,0:T(8,128)(2,1)}, bf16[704,1024]{1,0:T(8,128)(2,1)}, bf16[704,1024]{1,0:T(8,128)(2,1)}, bf16[256,1024]{1,0:T(8,128)(2,1)}, bf...) custom-call(bf16[256,1024]{1,0:T(8,128)(2,1)} %x_hbm.1, ...), custom_call_target="tpu_custom_call" | custom-call | tf_op jit(solution)/shard_map/pallas_call | solution.py:832
  200.0 7.4 %shard_map.221 = (f32[704,1024]{1,0:T(8,128)}, f32[704,1024]{1,0:T(8,128)}, f32[704,1024]{1,0:T(8,128)}, f32[256,1024]{1,0:T(8,128)}, f32[1024,256]{1,0:T(8,128)...) custom-call(bf16[704,1024]{1,0:T(8,128)(2,1)} %get-tuple-element.34., ...), custom_call_target="tpu_custom_call" | custom-call | tf_op jit(solution)/shard_map/pallas_call | solution.py:868
  207.4 1.4 fusion
